TPU v7x, 32 devices: a whole 2x2x4 slice. The times are simulated.
32 devices in a mesh: layer: 8 (over z, y), cuts: 4 (over x, core).
Axes of the slice: x: 2, y: 2, z: 4, core: 2. Of those that a mesh axis runs over, the one named last changes fastest.
Arguments:
- resid: bfloat16 [512, 2, 16384], P(None, None, 'cuts'), may hold values from -6 to 6
- enc_weight: bfloat16 [2, 16384, 2048], P(None, 'cuts', 'layer'), may hold values from -0.03125 to 0.03125
- enc_bias: float32 [2048], P('layer'), may hold values from -1 to 1
- dec_weight: bfloat16 [2048, 2, 16384], P('layer', None, 'cuts'), may hold values from -0.1875 to 0.1875
- dec_bias: float32 [2, 16384], P(None, 'cuts'), may hold values from -1 to 1
Outputs:
- enc_grad: bfloat16 [2, 16384, 2048], P(None, 'cuts', 'layer')
- dec_grad: bfloat16 [2048, 2, 16384], P('layer', None, 'cuts')
All inputs are finite; a program needn't handle non-finite values.
Results may differ from a plain program's by a relative error of at most 0.012.
Values may be sent and summed in bfloat16 or wider, within the bound.
No kernel may reach another device: no remote copies, remote signals or barrier semaphores. Data moves between devices by JAX's collectives and lax.ppermute only.
A program may use at most 128 MiB of HBM per device.

v0:
```python
import math

import jax
import jax.numpy as jnp
from jax import lax
from jax.sharding import PartitionSpec as P


def per_device(resid, enc_weight, enc_bias, dec_weight, dec_bias):
    rows = resid.shape[0]
    local = resid.reshape(rows, -1)
    width = local.shape[1]
    encoder = enc_weight.reshape(width, -1)
    feats = encoder.shape[1]
    decoder = dec_weight.reshape(feats, width)
    offset = dec_bias.reshape(-1)
    scale = 1.0 / math.sqrt(rows)
    groups = lax.axis_size("layer")
    partial_sum = jnp.dot(local, encoder, preferred_element_type=jnp.float32)
    z_local = lax.psum(partial_sum, "cuts") + enc_bias[None, :]
    act = jnp.maximum(z_local, 0.0).astype(jnp.bfloat16)
    share = rows // groups
    block = act
    recon = lax.psum_scatter(
        jnp.dot(block, decoder, preferred_element_type=jnp.float32),
        "layer",
        scatter_dimension=0,
        tiled=True,
    )
    mine = lax.axis_index("layer") * share
    own_rows = lax.dynamic_slice_in_dim(local, mine, share, 0)
    err = (recon + offset[None, :] - own_rows.astype(jnp.float32)).astype(jnp.bfloat16)
    piece = lax.all_gather(err, "layer", axis=0, tiled=True)
    block = act
    grad = lax.dot_general(
        block, piece, (((0,), (0,)), ((), ())), preferred_element_type=jnp.float32
    )
    values = lax.dot_general(
        piece, decoder, (((1,), (1,)), ((), ())), preferred_element_type=jnp.float32
    )
    dact = values
    grad, dact = (grad, dact)
    dec_grad = (grad * scale).astype(jnp.bfloat16)
    back = lax.psum(dact, "cuts")
    masked = jnp.where(z_local > 0, back * scale, 0.0).astype(jnp.bfloat16)
    enc_full = lax.dot_general(
        local, masked, (((0,), (0,)), ((), ())), preferred_element_type=jnp.float32
    )
    enc_grad = enc_full.astype(jnp.bfloat16).reshape(enc_weight.shape)
    return (enc_grad, dec_grad.reshape(dec_weight.shape))


def solution(mesh):
    placed = (
        P(None, None, "cuts"),
        P(None, "cuts", "layer"),
        P("layer"),
        P("layer", None, "cuts"),
        P(None, "cuts"),
    )
    return jax.shard_map(
        per_device,
        mesh=mesh,
        in_specs=placed,
        out_specs=(P(None, "cuts", "layer"), P("layer", None, "cuts")),
        check_vma=False,
    )
```

profile of v0, /device:TPU:0, one launch (start us, length us, event | category | flops | bytes accessed | tf_op | source)
XLA Modules:
  0.0 531.8 jit_solution(9085763619589539287)
XLA Ops:
  7.2 0.0 all-reduce.3.cloned.1.call-start
  7.2 10.1 %fusion.4 = f32[512,256]{1,0:T(8,128)} fusion(bf16[2,4096,256]{2,1,0:T(8,128)(2,1)} %param.6, bf16[512,2,4096]{2,1,0:T(2,128)(2,1)} %param.5), kind=kOutput, calls=%fused_computation.7 | convolution fusion | flops 2147483648 | bytes 13107200 | tf_op jit(solution)/shard_map/dot_general | solution.py:19
  17.3 0.0 all-reduce.3.cloned.1.call-update
  17.4 0.2 reduce-scatter.2.cloned.1.call-start
  17.6 0.0 copy-start.1
  17.6 8.7 %copy.10 = bf16[32,8,2,4096]{3,1,2,0:T(8,128)(2,1)} copy(bf16[32,8,2,4096]{3,2,1,0:T(2,128)(2,1)} %bitcast.22) | data formatting | bytes 8388608
  26.3 27.4 %all-reduce.3.cloned.1.call-done = f32[512,256]{1,0:T(8,128)} async-done(((f32[512,256]{1,0:T(8,128)}), f32[512,256]{1,0:T(8,128)}) %all-reduce.3.cloned.1.call-update) | async-done | bytes 524304 | tf_op jit(solution)/shard_map/psum | solution.py:20
  53.7 10.4 %fusion.10 = f32[512,8192]{1,0:T(8,128)} fusion(bf16[256,8192]{1,0:T(8,128)(2,1)} %bitcast.19, f32[512,256]{1,0:T(8,128)} %all-reduce.3.cloned.1.call-done, f32[256]{0:T(256)S(1)} %copy-done.1), kind=kOutput, calls=%fused_computation.13 | convolution fusion | flops 2147876864 | bytes 21496832 | tf_op jit(solution)/shard_map/dot_general | solution.py:25
  64.1 0.0 reduce-scatter.2.cloned.1.call-update
  64.1 0.3 all-gather.2.cloned.1.call-start
  64.4 0.0 copy-start.2
  64.4 16.2 %copy.12 = bf16[64,8,2,4096]{3,1,2,0:T(8,128)(2,1)} copy(bf16[64,8,2,4096]{3,2,1,0:T(2,128)(2,1)} %bitcast.21) | data formatting | bytes 16777216
  80.6 264.0 %reduce-scatter.2.cloned.1.call-done = f32[64,8192]{1,0:T(8,128)} async-done(((f32[512,8192]{1,0:T(8,128)}), f32[64,8192]{1,0:T(8,128)}) %reduce-scatter.2.cloned.1.call-update) | async-done | bytes 2097168 | tf_op jit(solution)/shard_map/reduce_scatter | solution.py:24
  344.6 3.1 subtract_convert_fusion
  347.7 0.0 all-gather.2.cloned.1.call-update
  347.7 0.3 all-reduce.5.cloned.1.call-start
  348.0 123.4 %all-gather.2.cloned.1.call-done = bf16[512,8192]{1,0:T(8,128)(2,1)} async-done(((bf16[64,8192]{1,0:T(8,128)(2,1)}), bf16[512,8192]{1,0:T(8,128)(2,1)}) %all-gather.2.cloned.1.call-update) | async-done | bytes 8388624 | tf_op jit(solution)/shard_map/all_gather | solution.py:33
  471.4 7.8 %fusion.15 = f32[512,256]{1,0:T(8,128)} fusion(bf16[512,8192]{1,0:T(8,128)(2,1)} %all-gather.2.cloned.1.call-done, bf16[256,8192]{1,0:T(8,128)(2,1)} %bitcast.20), kind=kOutput, calls=%fused_computation.18 | convolution fusion | flops 2147483648 | bytes 13107200 | tf_op jit(solution)/shard_map/dot_general | solution.py:38
  479.2 0.0 all-reduce.5.cloned.1.call-update
  479.2 7.8 %fusion = bf16[256,8192]{1,0:T(8,128)(2,1)} fusion(bf16[512,8192]{1,0:T(8,128)(2,1)} %all-gather.2.cloned.1.call-done, f32[512,256]{1,0:T(8,128)S(1)} %copy-done, f32[256]{0:T(256)S(1)} %copy-done.1), kind=kOutput, calls=%fused_computation.1 | convolution fusion | flops 2152071168 | bytes 13108224 | tf_op jit(solution)/shard_map/dot_general | solution.py:35
  487.0 7.8 %reshape.22 = bf16[256,2,4096]{2,1,0:T(2,128)(2,1)} reshape(bf16[256,8192]{1,0:T(8,128)(2,1)} %fusion) | data formatting | bytes 8388608 | tf_op jit(solution)/shard_map/reshape | solution.py:50
  494.9 16.1 %all-reduce.5.cloned.1.call-done = f32[512,256]{1,0:T(8,128)} async-done(((f32[512,256]{1,0:T(8,128)}), f32[512,256]{1,0:T(8,128)}) %all-reduce.5.cloned.1.call-update) | async-done | bytes 524304 | tf_op jit(solution)/shard_map/psum | solution.py:44
  511.0 7.9 %fusion.1 = bf16[8192,256]{0,1:T(8,128)(2,1)} fusion(bf16[512,8192]{1,0:T(8,128)(2,1)} %bitcast.18, f32[512,256]{1,0:T(8,128)} %all-reduce.5.cloned.1.call-done, f32[512,256]{1,0:T(8,128)S(1)} %copy-done, f32[256]{0:T(256)S(1)} %copy-done.1), kind=kOutput, calls=%fused_computation.3 | convolution fusion | flops 2150236160 | bytes 13632512 | tf_op jit(solution)/shard_map/dot_general | solution.py:46
  518.9 6.4 %copy.9 = bf16[8192,256]{1,0:T(8,128)(2,1)} copy(bf16[8192,256]{0,1:T(8,128)(2,1)} %fusion.1) | data formatting | bytes 8388608
  (5 shorter events, 0.0 us)
Async XLA Ops:
  7.2 46.5 %all-reduce.3.cloned.1.call-start = ((), (), s32[]{:S(2)}) async-start(), calls=%async_computation.1 | async-start | bytes 1048576 | tf_op jit(solution)/shard_map/psum | solution.py:20
  17.4 327.3 %reduce-scatter.2.cloned.1.call-start = ((), (), s32[]{:S(2)}) async-start(), calls=%async_computation.2 | async-start | bytes 18874368 | tf_op jit(solution)/shard_map/reduce_scatter | solution.py:24
  17.6 36.1 %copy-start.1 = (f32[256]{0:T(256)S(1)}, f32[256]{0:T(256)}, u32[]{:S(2)}) copy-start(f32[256]{0:T(256)} %param.7) | copy-start | bytes 3076
  64.1 407.3 %all-gather.2.cloned.1.call-start = ((), (), s32[]{:S(2)}) async-start(), calls=%async_computation.3 | async-start | bytes 9437184 | tf_op jit(solution)/shard_map/all_gather | solution.py:33
  64.4 16.2 %copy-start.2 = (f32[2,4096]{1,0:T(2,128)S(1)}, f32[2,4096]{1,0:T(2,128)}, u32[]{:S(2)}) copy-start(f32[2,4096]{1,0:T(2,128)} %param.9) | copy-start | bytes 98308
  347.7 131.5 %copy-start = (f32[512,256]{1,0:T(8,128)S(1)}, f32[512,256]{1,0:T(8,128)}, u32[]{:S(2)}) copy-start(f32[512,256]{1,0:T(8,128)} %all-reduce.3.cloned.1.call-done) | copy-start | bytes 1572868
  347.7 163.2 %all-reduce.5.cloned.1.call-start = ((), (), s32[]{:S(2)}) async-start(), calls=%async_computation.4 | async-start | bytes 1048576 | tf_op jit(solution)/shard_map/psum | solution.py:44
Sparse Core Ops, SparseCore 0:
  17.5 36.1 all-reduce.2
  64.2 280.3 reduce-scatter.1
  347.8 123.5 all-gather.1
  479.4 31.5 all-reduce.4
where the time goes:
time: 532 us
  waiting for transfers between devices  431 us (81%)
  matrix products  44 us (8%)
  local copies, waits for them, and re-layouts  39.1 us (7%)
  between operations  13.8 us (3%)
    reduce_scatter x1, waiting for transfers between devices, per_device(): lax.psum_scatter(jnp.dot(block, decoder, preferred_element_type=jnp.float...  264 us
    all_gather x1, waiting for transfers between devices, per_device(): piece = lax.all_gather(err, 'layer', axis=0, tiled=True)  123 us
    unnamed x10, local copies, waits for them, and re-layouts  31.3 us
    psum x1, waiting for transfers between devices, per_device(): z_local = lax.psum(partial_sum, 'cuts') + enc_bias[None, :]  27.4 us
    psum x1, waiting for transfers between devices, per_device(): back = lax.psum(dact, 'cuts')  16.1 us
  transfers between devices with their start and end apart: 4, of which 4 were waited for; matrix products, arithmetic and copies ran while one was open for 8% of the time, Pallas kernels for 0%

commit v1 on v0

v1 whole, which is shorter than its diff:
```python
import functools
import math

import jax
import jax.numpy as jnp
import numpy as np
from jax import lax
from jax.experimental import pallas as pl
from jax.experimental.pallas import tpu as pltpu
from jax.sharding import PartitionSpec as P


F32 = jnp.float32
BF16 = jnp.bfloat16
ENDS = 1
CHAINS = 2
FLATS = 4


def swap(value, axis, bit):
    size = lax.axis_size(axis)
    return lax.ppermute(value, axis, [(i, i ^ (1 << bit)) for i in range(size)])


def halves(value, upper):
    half = value.shape[0] // 2
    low, high = value[:half], value[half:]
    return jnp.where(upper, high, low), jnp.where(upper, low, high)


def joined(mine, theirs, upper):
    return jnp.where(
        upper,
        jnp.concatenate([theirs, mine], 0),
        jnp.concatenate([mine, theirs], 0),
    )


def dot(a, b, dims):
    return lax.dot_general(a, b, (dims, ((), ())), preferred_element_type=F32)


def limits(mib):
    return pltpu.CompilerParams(vmem_limit_bytes=mib << 20)


def cost(flops, moved):
    return pl.CostEstimate(flops=flops, bytes_accessed=moved, transcendentals=0)


def enc_grad_kernel(*refs):
    *rows, dz, out = refs
    left = jnp.concatenate([r[0] for r in rows], 0)
    out[0] = dot(left, dz[...], ((0,), (0,))).astype(out.dtype)


def enc_grad_of(rows, dz, blocks):
    layers, size, width = rows[0].shape
    tokens, feats = dz.shape
    block = width // blocks
    return pl.pallas_call(
        enc_grad_kernel,
        grid=(layers, blocks),
        in_specs=[pl.BlockSpec((1, size, block), lambda l, i: (l, 0, i)) for _ in rows]
        + [pl.BlockSpec(dz.shape, lambda l, i: (0, 0))],
        out_specs=pl.BlockSpec((1, block, feats), lambda l, i: (l, i, 0)),
        out_shape=jax.ShapeDtypeStruct((layers, width, feats), BF16),
        compiler_params=limits(24),
        cost_estimate=cost(
            2 * tokens * layers * width * feats, 2 * layers * width * (tokens + feats)
        ),
    )(*rows, dz)


def prep_kernel(table, rows, out):
    _, units, feats, cols = out.shape
    layers = rows.shape[1]
    part = cols // layers
    size = feats * layers
    to = lax.broadcasted_iota(jnp.int32, (size, size), 0)
    at = lax.broadcasted_iota(jnp.int32, (size, size), 1)
    order = jnp.where(at == layers * (to % feats) + to // feats, 1.0, 0.0).astype(BF16)
    flat = rows[...].reshape(size, units * part)
    flat = dot(order, flat, ((1,), (0,))).astype(BF16)
    for u in range(units):
        for layer in range(layers):
            out[0, u, :, layer * part : (layer + 1) * part] = flat[
                layer * feats : (layer + 1) * feats, u * part : (u + 1) * part
            ]


def prep(weight, table, at, count, span, units, room=16):
    feats, layers, _ = weight.shape
    cols = layers * span // units
    return pl.pallas_call(
        prep_kernel,
        grid_spec=pltpu.PrefetchScalarGridSpec(
            num_scalar_prefetch=1,
            grid=(count,),
            in_specs=[
                pl.BlockSpec((feats, layers, span), lambda i, t: (0, 0, t[at + i]))
            ],
            out_specs=pl.BlockSpec((1, units, feats, cols), lambda i, t: (i, 0, 0, 0)),
        ),
        out_shape=jax.ShapeDtypeStruct((count, units, feats, cols), BF16),
        compiler_params=limits(room),
        cost_estimate=cost(0, 4 * count * feats * layers * span),
    )(table, weight)


def place_kernel(starts, table, *refs):
    out = refs[-1]
    part = out.shape[2]
    step = pl.program_id(0)
    for j in range(len(starts) - 1):

        @pl.when((step >= starts[j]) & (step < starts[j + 1]))
        def _(ref=refs[j]):
            for layer in range(out.shape[1]):
                out[:, layer, :] = ref[0, :, layer * part : (layer + 1) * part]


def place(groups, table, at, shape, held):
    feats, layers, _ = shape
    cols = groups[0].shape[2]
    part = cols // layers
    starts = [0]
    for g in groups:
        starts.append(starts[-1] + g.shape[0])

    def spec(j):
        most = groups[j].shape[0] - 1

        def index(i, t):
            return (jnp.clip(i - starts[j], 0, most), 0, 0)

        return pl.BlockSpec((1, feats, cols), index)

    specs = [spec(j) for j in range(len(groups))]
    operands = list(groups)
    aliases = {}
    if held is not None:
        specs.append(pl.BlockSpec(memory_space=pl.ANY))
        operands.append(held)
        aliases = {len(operands): 0}
    return pl.pallas_call(
        functools.partial(place_kernel, starts),
        grid_spec=pltpu.PrefetchScalarGridSpec(
            num_scalar_prefetch=1,
            grid=(starts[-1],),
            in_specs=specs,
            out_specs=pl.BlockSpec(
                (feats, layers, part), lambda i, t: (0, 0, t[at + i])
            ),
        ),
        out_shape=jax.ShapeDtypeStruct(shape, BF16),
        input_output_aliases=aliases,
        compiler_params=limits(16),
        cost_estimate=cost(0, 4 * starts[-1] * feats * cols),
    )(table, *operands)


def goal_kernel(table, resid, bias, out):
    part = resid.shape[2]
    for layer in range(resid.shape[1]):
        rows = resid[:, layer, :].astype(F32)
        out[0, :, layer * part : (layer + 1) * part] = bias[layer][None, :] - rows


def goals_of(resid, bias, table, at, count, part):
    tokens, layers, _ = resid.shape
    return pl.pallas_call(
        goal_kernel,
        grid_spec=pltpu.PrefetchScalarGridSpec(
            num_scalar_prefetch=1,
            grid=(count,),
            in_specs=[
                pl.BlockSpec((tokens, layers, part), lambda i, t: (0, 0, t[at + i])),
                pl.BlockSpec((layers, part), lambda i, t: (0, t[at + i])),
            ],
            out_specs=pl.BlockSpec((1, tokens, layers * part), lambda i, t: (i, 0, 0)),
        ),
        out_shape=jax.ShapeDtypeStruct((count, tokens, layers * part), F32),
        compiler_params=limits(12),
        cost_estimate=cost(0, 6 * count * tokens * layers * part),
    )(table, resid, bias)


def flat_kernel(rows, out):
    layers, count, block = out.shape
    size = count * layers
    to = lax.broadcasted_iota(jnp.int32, (size, size), 0)
    at = lax.broadcasted_iota(jnp.int32, (size, size), 1)
    order = jnp.where(at == layers * (to % count) + to // count, 1.0, 0.0).astype(BF16)
    flat = dot(order, rows[...].reshape(size, block), ((1,), (0,))).astype(BF16)
    for layer in range(layers):
        out[layer] = flat[layer * count : (layer + 1) * count]


def flat_of(resid, piece, pieces, blocks):
    tokens, layers, width = resid.shape
    size, block = tokens // pieces, width // blocks
    return pl.pallas_call(
        flat_kernel,
        grid=(blocks,),
        in_specs=[pl.BlockSpec((size, layers, block), lambda i: (piece, 0, i))],
        out_specs=pl.BlockSpec((layers, size, block), lambda i: (0, 0, i)),
        out_shape=jax.ShapeDtypeStruct((layers, size, width), BF16),
        compiler_params=limits(12),
        cost_estimate=cost(0, 4 * size * layers * width),
    )(resid)


def use_kernel(n, scale, at, has_sum, table, act_t, weights, *refs):
    errs, rest = refs[:n], refs[n:]
    near, far, total = rest[-3:]
    step = pl.program_id(0)
    base = at + 4 * step
    src, valid = table[base], table[base + 2]
    if n == 1:
        e = errs[0][...]
    else:
        e = jnp.where(src == 0, errs[0][...], errs[1][...])
        for j in range(2, n):
            e = jnp.where(src == j, errs[j][...], e)
    feats, layers, part = near.shape
    grad = (dot(act_t[...], e, ((1,), (0,))) * scale).astype(BF16)
    for layer in range(layers):
        near[:, layer, :] = grad[:feats, layer * part : (layer + 1) * part]
    far[0] = grad[feats:]
    more = dot(e, weights[0], ((1,), (1,))) * valid.astype(F32)

    @pl.when(step == 0)
    def _():
        total[...] = rest[0][...] + more if has_sum else more

    @pl.when(step > 0)
    def _():
        total[...] += more


def use_of(act_t, weights, errs, total, held, table, at, m, shape, scale):
    feats, layers, _ = shape
    _, double, cols = weights.shape
    tokens = act_t.shape[1]
    part = cols // layers
    whole = lambda a: pl.BlockSpec(a.shape, lambda i, t: (0, 0))
    specs = [
        whole(act_t),
        pl.BlockSpec((1, double, cols), lambda i, t: (t[at + 4 * i + 1], 0, 0)),
        *[whole(e) for e in errs],
    ]
    operands = [act_t, weights, *errs]
    aliases = {}
    if total is not None:
        specs.append(whole(total))
        operands.append(total)
        aliases[len(operands)] = 2
    if held is not None:
        specs.append(pl.BlockSpec(memory_space=pl.ANY))
        operands.append(held)
        aliases[len(operands)] = 0
    body = functools.partial(use_kernel, len(errs), scale, at, total is not None)
    return pl.pallas_call(
        body,
        grid_spec=pltpu.PrefetchScalarGridSpec(
            num_scalar_prefetch=1,
            grid=(m,),
            in_specs=specs,
            out_specs=[
                pl.BlockSpec(
                    (feats, layers, part), lambda i, t: (0, 0, t[at + 4 * i + 3])
                ),
                pl.BlockSpec((1, feats, cols), lambda i, t: (i, 0, 0)),
                pl.BlockSpec((tokens, double), lambda i, t: (0, 0)),
            ],
        ),
        out_shape=[
            jax.ShapeDtypeStruct(shape, BF16),
            jax.ShapeDtypeStruct((m, feats, cols), BF16),
            jax.ShapeDtypeStruct((tokens, double), F32),
        ],
        input_output_aliases=aliases,
        compiler_params=limits(24),
        cost_estimate=cost(
            4 * m * tokens * double * cols, 2 * m * cols * (tokens + 2 * double)
        ),
    )(table, *operands)


def groups_of(units, steps):
    groups = [[(0, 0)]]
    for s in range(1, steps + 1):
        groups.append([(s, -1), (s, 1)] if 2 * s < units else [(s, 0)])
    return groups


def turn_kernel(rows, out):
    out[...] = rows[...].T


def turned(rows):
    return pl.pallas_call(
        turn_kernel,
        out_shape=jax.ShapeDtypeStruct(rows.shape[::-1], rows.dtype),
        compiler_params=limits(12),
        cost_estimate=cost(0, 4 * rows.size),
    )(rows)


def tables(line, ends, units, steps, chains):
    groups = groups_of(units, steps)
    rows = []
    for spot in range(2 * line):
        pos, side = divmod(spot, 2)
        centre = pos + ends - 1

        def taken(s, d):
            if d or not s:
                return d, (centre + d * s) % units, 1
            if centre - s >= 0:
                return -1, centre - s, 1
            if centre + s < units:
                return 1, centre + s, 1
            return 0, centre, 0

        row, at = [], {}

        def add(name, values):
            at[name] = len(row)
            row.extend(values)

        add("prep_a", [(1 - side) * chains])
        add("prep_b", [side * chains])
        add(
            "prep_c",
            [of * chains + k for of in (1 - side, side) for k in range(1, chains)],
        )
        sign = -1 if pos < line // 2 else 1
        add(
            "goals",
            [
                (side * chains + k) * units + centre + sign * e
                for k in range(chains)
                for e in range(ends)
            ],
        )
        for k in range(chains):
            base = (side * chains + k) * units
            for i, group in enumerate(groups):
                values = []
                came = [e for e in group if e[0]]
                for s, d in group:
                    way, unit, valid = taken(s, d)
                    src = 0
                    if way:
                        src = 1 + 2 * sorted({e[0] for e in came}).index(s) + (way > 0)
                    values += [src, unit, valid, base + unit]
                add(f"use_{k}_{i}", values)
        far = [
            [
                [((1 - side) * chains + k) * units + taken(s, d)[1] for s, d in group]
                for group in groups
            ]
            for k in range(chains)
        ]
        for k in range(chains):
            add(f"far_{k}", sum(far[k][:-1], []))
        add("far_last", sum((far[k][-1] for k in range(chains)), []))
        rows.append(row)
    return np.array(rows, np.int32), at


def microstep(resid, enc_weight, enc_bias, dec_weight, dec_bias):
    tokens, _, width = resid.shape
    feats = enc_weight.shape[2]
    scale = 1.0 / math.sqrt(tokens)
    n_cuts = lax.axis_size("cuts")
    bits = n_cuts.bit_length() - 1
    line = lax.axis_size("layer") // 2
    spot = lax.axis_index("layer")
    pos = spot // 2
    cut = lax.axis_index("cuts")
    ups = [(cut >> b) % 2 == 1 for b in range(bits)]
    half = width // 2
    ends = ENDS if half % (128 * (line - 2 + 2 * ENDS)) == 0 else 1
    units = line - 2 + 2 * ends
    steps = line - 2 + ends
    chains = CHAINS
    while chains > 1 and half % (128 * units * chains):
        chains //= 2
    span = half // chains
    part = span // units
    centre = pos + ends - 1
    rows, at = tables(line, ends, units, steps, chains)
    table = lax.dynamic_index_in_dim(jnp.asarray(rows), spot, 0, keepdims=False)

    give = prep(dec_weight, table, at["prep_a"], 1, span, units, 60)
    got = [swap(give[0], "layer", 0)]

    z = dot(resid.reshape(tokens, -1), enc_weight.reshape(-1, feats), ((1,), (0,)))
    held = prep(dec_weight, table, at["prep_b"], 1, span, units)
    own = [held[0]]
    for b in range(bits):
        stay, go = halves(z, ups[b])
        come = swap(go, "cuts", b)
        z = stay + come
    act_mine = jnp.maximum(z + enc_bias[None, :], 0.0).astype(BF16)
    come = swap(act_mine, "layer", 0)
    for k in range(1, chains):
        held = prep(dec_weight, table, at["prep_c"] + k - 1, 1, span, units)
        got.append(swap(held[0], "layer", 0))
        held = prep(dec_weight, table, at["prep_c"] + chains + k - 2, 1, span, units)
        own.append(held[0])
    act = jnp.concatenate([act_mine, come], 1)
    for b in reversed(range(bits)):
        come = swap(act, "cuts", b)
        act = joined(act, come, ups[b])
    goals = goals_of(resid, dec_bias, table, at["goals"], chains * ends, part)

    def shift(value, step, sources):
        pairs = [
            (2 * i + s, 2 * (i + step) + s)
            for i in sources
            if 0 <= i < line and 0 <= i + step < line
            for s in range(2)
        ]
        return lax.ppermute(value, "layer", pairs)

    both = [
        lax.optimization_barrier(jnp.concatenate([own[k], got[k]], 1))
        for k in range(chains)
    ]
    act_t = turned(act)

    def weights(k, u):
        return lax.dynamic_index_in_dim(both[k], u, 0, keepdims=False)

    def recon(k, u):
        return dot(act, weights(k, u), ((1,), (0,)))

    right, left = [None] * chains, [None] * chains
    errs = [[None] * ends for _ in range(chains)]
    for s in range(1, steps + 1):
        for k in range(chains):
            r = recon(k, jnp.clip(units - s + pos, 0, units - 1))
            l = recon(k, jnp.clip(s - line + pos, 0, units - 1))
            if s > 1:
                r = r + right[k].astype(F32)
                l = l + left[k].astype(F32)
            right[k] = shift(r.astype(BF16), 1, range(0, s))
            left[k] = shift(l.astype(BF16), -1, range(line - s, line))
            late = steps - s
            if late < ends:
                u = jnp.where(pos < line // 2, centre - late, centre + late)
                err = recon(k, u) + right[k].astype(F32) + left[k].astype(F32)
                err = err + goals[k * ends + late]
                errs[k][late] = err.astype(BF16)

    dact = dec_grad = None
    fars = [[] for _ in range(chains)]
    groups = groups_of(units, steps)
    right = [errs[k][0] for k in range(chains)]
    left = [errs[k][0] for k in range(chains)]
    came = [[] for _ in range(chains)]

    def put(name, which, dec_grad):
        return place(which, table, at[name], dec_weight.shape, dec_grad)

    for s in range(steps + 1):
        for k in range(chains if s else 0):
            right[k] = shift(right[k], 1, range(max(s - ends, 0), line - 1))
            left[k] = shift(
                left[k], -1, range(1, min(line - 1 + ends - s, line - 1) + 1)
            )
            if s < ends:
                right[k] = jnp.where(pos == 0, errs[k][s], right[k])
                left[k] = jnp.where(pos == line - 1, errs[k][s], left[k])
            came[k] += [right[k], left[k]]
        for k in range(chains):
            for i, group in enumerate(groups):
                if group[-1][0] != s:
                    continue
                if i == len(groups) - 1 and k == chains - 1:
                    for c in range(chains):
                        dec_grad = put(f"far_{c}", fars[c][:i], dec_grad)
                dec_grad, far, dact = use_of(
                    act_t,
                    both[k],
                    [errs[k][0], *came[k]],
                    dact,
                    dec_grad,
                    table,
                    at[f"use_{k}_{i}"],
                    len(group),
                    dec_weight.shape,
                    scale,
                )
                came[k] = []
                fars[k].append(swap(far, "layer", 0))
    dec_grad = put("far_last", [f[-1] for f in fars], dec_grad)

    flats = []
    for i in range(FLATS):
        flats.append(flat_of(resid, i, FLATS, 4))

    for b in range(bits):
        stay, go = halves(dact, ups[b])
        come = swap(go.astype(BF16), "cuts", b).astype(F32)
        dact = stay + come
    come = swap(dact[:, feats:].astype(BF16), "layer", 0).astype(F32)
    dact = dact[:, :feats] + come
    dz = jnp.where(act_mine > 0, dact * scale, 0.0).astype(BF16)
    for b in reversed(range(bits)):
        come = swap(dz, "cuts", b)
        dz = joined(dz, come, ups[b])
    enc_grad = enc_grad_of(flats, dz, 2)
    return enc_grad, dec_grad


def solution(mesh):
    placed = (
        P(None, None, "cuts"),
        P(None, "cuts", "layer"),
        P("layer"),
        P("layer", None, "cuts"),
        P(None, "cuts"),
    )
    return jax.shard_map(
        microstep,
        mesh=mesh,
        in_specs=placed,
        out_specs=(P(None, "cuts", "layer"), P("layer", None, "cuts")),
        check_vma=False,
    )
```

time: 532 us -> 252 us (0.47)
  waiting for transfers between devices: 431 us -> 91.7 us
  starting transfers between devices: 0.83 us -> 69.6 us
  Pallas kernels: 0 us -> 49.9 us
  local copies, waits for them, and re-layouts: 39.1 us -> 13.5 us
  matrix products: 44 us -> 21.1 us
  between operations: 13.8 us -> 1.32 us
    reduce_scatter x1 -> x0, waiting for transfers between devices: 264 us -> none  [per_device(): lax.psum_scatter(jnp.dot(block, decoder, preferred_element_type=jnp.float...]
    all_gather x1 -> x0, waiting for transfers between devices: 123 us -> none  [per_device(): piece = lax.all_gather(err, 'layer', axis=0, tiled=True)]
    ppermute x0 -> x44, waiting for transfers between devices: none -> 91.7 us  [the longest x20 53 us: swap(): return lax.ppermute(value, axis, [(i, i ^ 1 << bit) for i in range(size)])]
    ppermute x0 -> x44, starting transfers between devices: none -> 69.6 us  [the longest x24 48.9 us: shift(): return lax.ppermute(value, 'layer', pairs)]
    pallas_call x0 -> x22, Pallas kernels: none -> 49.9 us  [the longest x8 18.8 us: use_of(): pl.pallas_call(body, grid_spec=pltpu.PrefetchScalarGridSpec(num_scalar_pr...]
    psum x2 -> x0, waiting for transfers between devices: 43.5 us -> none  [the longest x1 27.4 us: per_device(): z_local = lax.psum(partial_sum, 'cuts') + enc_bias[None, :]]
    dot_general x5 -> x15, matrix products: 44 us -> 21.1 us  [dot(): return lax.dot_general(a, b, (dims, ((), ())), preferred_element_type=F32)]
    unnamed x10 -> x30, local copies, waits for them, and re-layouts: 31.3 us -> 12.2 us
  transfers between devices with their start and end apart: 4 -> 44, of which waited for: 4 -> 19; matrix products, arithmetic and copies ran while one was open for 8% -> 6% of each run, Pallas kernels for 0% -> 17%
where the time goes in v1:
time: 252 us; the launch traced here: 251 us
  waiting for transfers between devices  91.7 us (36%)
  starting transfers between devices  69.6 us (28%)
  Pallas kernels  49.9 us (20%)
  matrix products  21.1 us (8%)
  local copies, waits for them, and re-layouts  13.5 us (5%)
  other arithmetic  3.55 us (1%)
    ppermute x20, waiting for transfers between devices, swap(): return lax.ppermute(value, axis, [(i, i ^ 1 << bit) for i in range(size)])  53 us
    ppermute x24, starting transfers between devices, shift(): return lax.ppermute(value, 'layer', pairs)  48.9 us
    ppermute x24, waiting for transfers between devices, shift(): return lax.ppermute(value, 'layer', pairs)  38.8 us
    dot_general x15, matrix products, dot(): return lax.dot_general(a, b, (dims, ((), ())), preferred_element_type=F32)  21.1 us
    ppermute x20, starting transfers between devices, swap(): return lax.ppermute(value, axis, [(i, i ^ 1 << bit) for i in range(size)])  20.7 us
    pallas_call x8, Pallas kernels, use_of(): pl.pallas_call(body, grid_spec=pltpu.PrefetchScalarGridSpec(num_scalar_pr...  18.8 us
    unnamed x30, local copies, waits for them, and re-layouts  12.2 us
    pallas_call x3, Pallas kernels, place(): pl.pallas_call(functools.partial(place_kernel, starts), grid_spec=pltpu.P...  9.14 us
  transfers between devices with their start and end apart: 44, of which 19 were waited for; matrix products, arithmetic and copies ran while one was open for 6% of the time, Pallas kernels for 17%

profile of v1, /device:TPU:0, one launch (start us, length us, event | category | flops | bytes accessed | tf_op | source)
XLA Modules:
  0.0 250.6 jit_solution(10160976315612281425)
XLA Ops:
  0.6 9.3 %fusion.16 = f32[512,256]{1,0:T(8,128)S(1)} fusion(bf16[2,4096,256]{2,1,0:T(8,128)(2,1)} %param.7, bf16[512,2,4096]{2,1,0:T(2,128)(2,1)} %resid.1), kind=kOutput, calls=%fused_computation.32 | convolution fusion | flops 2147483648 | bytes 13107200 | tf_op jit(solution)/shard_map/dot_general | solution.py:40
  15.9 3.7 %shard_map.86 = bf16[1,4,256,512]{3,2,1,0:T(8,128)(2,1)} custom-call(s32[56]{0:T(128)} %fusion.64.table, bf16[256,2,4096]{2,1,0:T(2,128)(2,1)} %rows.15), custom_call_target="tpu_custom_call" | custom-call | bytes 2097152 | tf_op jit(solution)/shard_map/pallas_call | solution.py:95
  21.8 24.4 %collective-permute-done.2 = bf16[128,256]{1,0:T(8,128)(2,1)S(1)} collective-permute-done((bf16[128,256]{1,0:T(8,128)(2,1)S(1)}, bf16[128,256]{1,0:T(8,128)(2,1)S(1)}, u32[]{:S(2)}, u32[]{:S(2)}) %collective-permute-start.2) | collective-permute-done | bytes 65568 | tf_op jit(solution)/shard_map/ppermute | solution.py:22
  46.6 4.7 %collective-permute-done.3 = bf16[128,512]{1,0:T(8,128)(2,1)S(1)} collective-permute-done((bf16[128,512]{1,0:T(8,128)(2,1)S(1)}, bf16[128,512]{1,0:T(8,128)(2,1)S(1)}, u32[]{:S(2)}, u32[]{:S(2)}) %collective-permute-start.3) | collective-permute-done | bytes 131104 | tf_op jit(solution)/shard_map/ppermute | solution.py:22
  66.6 3.6 %collective-permute-start.19 = (bf16[512,512]{1,0:T(8,128)(2,1)S(1)}, bf16[512,512]{1,0:T(8,128)(2,1)S(1)}, u32[]{:S(2)}, u32[]{:S(2)}) collective-permute-start(bf16[512,512]{1,0:T(8,128)(2,1)S(1)} %convolution_convert_fusion.1), channel_id=1, source_target_pairs={{0,8},{4,12},{1,9},{5,13},{2,10},{6,14},{3,11},{7,15}} | collective-permute-start | bytes 1572872 | tf_op jit(solution)/shard_map/ppermute | solution.py:428
  71.4 9.2 %collective-permute-done.5 = bf16[4,256,512]{2,1,0:T(8,128)(2,1)} collective-permute-done((bf16[4,256,512]{2,1,0:T(8,128)(2,1)S(1)}, bf16[4,256,512]{2,1,0:T(8,128)(2,1)}, u32[]{:S(2)}, u32[]{:S(2)}) %collective-permute-start.5) | collective-permute-done | bytes 1048608 | tf_op jit(solution)/shard_map/ppermute | solution.py:22
  82.4 3.5 %collective-permute-start.6 = (bf16[512,512]{1,0:T(8,128)(2,1)S(1)}, bf16[512,512]{1,0:T(8,128)(2,1)S(1)}, u32[]{:S(2)}, u32[]{:S(2)}) collective-permute-start(bf16[512,512]{1,0:T(8,128)(2,1)S(1)} %convolution_convert_fusion.3), channel_id=1, source_target_pairs={{0,8},{4,12},{1,9},{5,13},{2,10},{6,14},{3,11},{7,15}} | collective-permute-start | bytes 1572872 | tf_op jit(solution)/shard_map/ppermute | solution.py:428
  90.1 8.2 %collective-permute-done.6 = bf16[512,512]{1,0:T(8,128)(2,1)S(1)} collective-permute-done((bf16[512,512]{1,0:T(8,128)(2,1)S(1)}, bf16[512,512]{1,0:T(8,128)(2,1)S(1)}, u32[]{:S(2)}, u32[]{:S(2)}) %collective-permute-start.6) | collective-permute-done | bytes 524320 | tf_op jit(solution)/shard_map/ppermute | solution.py:428
  98.7 4.4 %collective-permute-start.7 = (bf16[512,512]{1,0:T(8,128)(2,1)S(1)}, bf16[512,512]{1,0:T(8,128)(2,1)S(1)}, u32[]{:S(2)}, u32[]{:S(2)}) collective-permute-start(bf16[512,512]{1,0:T(8,128)(2,1)S(1)} %fusion.8), channel_id=1, source_target_pairs={{0,8},{4,12},{8,16},{12,20},{1,9},{5,13},{9,17},{13,21},{2,10},{6,... | collective-permute-start | bytes 1572872 | tf_op jit(solution)/shard_map/ppermute | solution.py:428
  104.4 5.0 %collective-permute-done.20 = bf16[512,512]{1,0:T(8,128)(2,1)S(1)} collective-permute-done((bf16[512,512]{1,0:T(8,128)(2,1)S(1)}, bf16[512,512]{1,0:T(8,128)(2,1)S(1)}, u32[]{:S(2)}, u32[]{:S(2)}) %collective-permute-start.20) | collective-permute-done | bytes 524320 | tf_op jit(solution)/shard_map/ppermute | solution.py:428
  109.9 5.2 %collective-permute-start.21 = (bf16[512,512]{1,0:T(8,128)(2,1)S(1)}, bf16[512,512]{1,0:T(8,128)(2,1)}, u32[]{:S(2)}, u32[]{:S(2)}) collective-permute-start(bf16[512,512]{1,0:T(8,128)(2,1)S(1)} %fusion.12), channel_id=1, source_target_pairs={{0,8},{4,12},{8,16},{12,20},{16,24},{20,28},{1,9},{5,13},{9,17},{1... | collective-permute-start | bytes 1572872 | tf_op jit(solution)/shard_map/ppermute | solution.py:428
  121.9 5.2 %collective-permute-start.8 = (bf16[512,512]{1,0:T(8,128)(2,1)}, bf16[512,512]{1,0:T(8,128)(2,1)}, u32[]{:S(2)}, u32[]{:S(2)}) collective-permute-start(bf16[512,512]{1,0:T(8,128)(2,1)} %fusion.7), channel_id=1, source_target_pairs={{0,8},{4,12},{8,16},{12,20},{16,24},{20,28},{1,9},{5,13},{9,17},{1... | collective-permute-start | bytes 1572872 | tf_op jit(solution)/shard_map/ppermute | solution.py:428
  139.1 4.7 %collective-permute-start.25 = (bf16[512,512]{1,0:T(8,128)(2,1)S(1)}, bf16[512,512]{1,0:T(8,128)(2,1)S(1)}, u32[]{:S(2)}, u32[]{:S(2)}) collective-permute-start(bf16[512,512]{1,0:T(8,128)(2,1)S(1)} %fusion.11.refs_0_), channel_id=1, source_target_pairs={{0,8},{4,12},{8,16},{12,20},{16,24},{20,28},{1,9},{5,13},{9,17},{1... | collective-permute-start | bytes 1572872 | tf_op jit(solution)/shard_map/ppermute | solution.py:428
  146.9 4.6 %collective-permute-start.12 = (bf16[512,512]{1,0:T(8,128)(2,1)S(1)}, bf16[512,512]{1,0:T(8,128)(2,1)S(1)}, u32[]{:S(2)}, u32[]{:S(2)}) collective-permute-start(bf16[512,512]{1,0:T(8,128)(2,1)S(1)} %fusion.6.refs_0_), channel_id=1, source_target_pairs={{0,8},{4,12},{8,16},{12,20},{16,24},{20,28},{1,9},{5,13},{9,17},{1... | collective-permute-start | bytes 1572872 | tf_op jit(solution)/shard_map/ppermute | solution.py:428
  156.8 3.5 %collective-permute-done.28.refs_2_ = bf16[512,512]{1,0:T(8,128)(2,1)S(1)} collective-permute-done((bf16[512,512]{1,0:T(8,128)(2,1)S(1)}, bf16[512,512]{1,0:T(8,128)(2,1)S(1)}, u32[]{:S(2)}, u32[]{:S(2)}) %collective-permute-start.28) | collective-permute-done | bytes 524320 | tf_op jit(solution)/shard_map/ppermute | solution.py:428
  167.8 3.8 %collective-permute-done.15.refs_2_ = bf16[512,512]{1,0:T(8,128)(2,1)S(1)} collective-permute-done((bf16[512,512]{1,0:T(8,128)(2,1)S(1)}, bf16[512,512]{1,0:T(8,128)(2,1)S(1)}, u32[]{:S(2)}, u32[]{:S(2)}) %collective-permute-start.15) | collective-permute-done | bytes 524320 | tf_op jit(solution)/shard_map/ppermute | solution.py:428
  172.8 3.4 %shard_map.89 = (bf16[256,2,4096]{2,1,0:T(2,128)(2,1)}, bf16[2,256,512]{2,1,0:T(8,128)(2,1)S(1)}, f32[512,512]{1,0:T(8,128)S(1)}) custom-call(s32[56]{0:T(128)S(1)} %copy-done.10, bf16[512,512]{1,0:T(8,128)(2,1)S(1)} %shard_map.81.act_t, bf16[4,512,512]{2,1,0:T(8,128)(2,1)S(1)} %copy-done.2, ...), custom_call_target="tpu_custom_call", output_to_operand_aliasing={{2}: (6, {}), {0}: (7, {})} | custom-call | flops 1073741824 | bytes 3145728 | tf_op jit(solution)/shard_map/pallas_call | solution.py:264
  177.8 3.4 %shard_map.90 = (bf16[256,2,4096]{2,1,0:T(2,128)(2,1)}, bf16[2,256,512]{2,1,0:T(8,128)(2,1)S(1)}, f32[512,512]{1,0:T(8,128)S(1)}) custom-call(s32[56]{0:T(128)S(1)} %copy-done.10, bf16[512,512]{1,0:T(8,128)(2,1)S(1)} %shard_map.81.act_t, bf16[4,512,512]{2,1,0:T(8,128)(2,1)S(1)} %pad_maximum_fusion.weights, ...), custom_call_target="tpu_custom_call", output_to_operand_aliasing={{2}: (6, {}), {0}: (7, {})} | custom-call | flops 1073741824 | bytes 3145728 | tf_op jit(solution)/shard_map/pallas_call | solution.py:264
  187.6 6.4 %collective-permute-done.16.refs_2_ = bf16[512,512]{1,0:T(8,128)(2,1)S(1)} collective-permute-done((bf16[512,512]{1,0:T(8,128)(2,1)S(1)}, bf16[512,512]{1,0:T(8,128)(2,1)S(1)}, u32[]{:S(2)}, u32[]{:S(2)}) %collective-permute-start.16) | collective-permute-done | bytes 524320 | tf_op jit(solution)/shard_map/ppermute | solution.py:428
  200.3 4.9 %collective-permute-done.30.refs_2_ = bf16[512,512]{1,0:T(8,128)(2,1)S(1)} collective-permute-done((bf16[512,512]{1,0:T(8,128)(2,1)S(1)}, bf16[512,512]{1,0:T(8,128)(2,1)S(1)}, u32[]{:S(2)}, u32[]{:S(2)}) %collective-permute-start.30) | collective-permute-done | bytes 524320 | tf_op jit(solution)/shard_map/ppermute | solution.py:428
  208.7 3.4 %shard_map.94.refs_3_ = bf16[256,2,4096]{2,1,0:T(2,128)(2,1)} custom-call(s32[56]{0:T(128)S(1)} %copy-done.10, bf16[1,256,512]{2,1,0:T(8,128)(2,1)S(1)} %collective-permute-done.34.refs_0_, bf16[2,256,512]{2,1,0:T(8,128)(2,1)S(1)} %collective-permute-done.35.refs_1_, ...), custom_call_target="tpu_custom_call", output_to_operand_aliasing={{}: (4, {})} | custom-call | bytes 2097152 | tf_op jit(solution)/shard_map/pallas_call | solution.py:146
  213.7 3.4 %shard_map.95.refs_4_ = bf16[256,2,4096]{2,1,0:T(2,128)(2,1)} custom-call(s32[56]{0:T(128)S(1)} %copy-done.10, bf16[1,256,512]{2,1,0:T(8,128)(2,1)S(1)} %collective-permute-done.31.refs_0_, bf16[2,256,512]{2,1,0:T(8,128)(2,1)S(1)} %collective-permute-done.32.refs_1_, ...), custom_call_target="tpu_custom_call", output_to_operand_aliasing={{}: (4, {})} | custom-call | bytes 2097152 | tf_op jit(solution)/shard_map/pallas_call | solution.py:146
  221.6 5.0 %collective-permute-done.38 = bf16[128,512]{1,0:T(8,128)(2,1)S(1)} collective-permute-done((bf16[128,512]{1,0:T(8,128)(2,1)S(1)}, bf16[128,512]{1,0:T(8,128)(2,1)S(1)}, u32[]{:S(2)}, u32[]{:S(2)}) %collective-permute-start.38) | collective-permute-done | bytes 131104 | tf_op jit(solution)/shard_map/ppermute | solution.py:22
  245.7 4.9 %shard_map.97 = bf16[2,4096,256]{2,1,0:T(8,128)(2,1)} custom-call(bf16[2,128,4096]{2,1,0:T(8,128)(2,1)S(1)} %shard_map.77.refs_0_, bf16[2,128,4096]{2,1,0:T(8,128)(2,1)S(1)} %shard_map.78.refs_1_, bf16[2,128,4096]{2,1,0:T(8,128)(2,1)S(1)} %shard_map.79.refs_2_, bf16[2,128,4096]{2,1,0:T(8,128)(2,1)S(1)} %shard_map.80.refs_3_, ...), custom_call_target="tpu_custom_call" | custom-call | flops 2147483648 | bytes 12582912 | tf_op jit(solution)/shard_map/pallas_call | solution.py:61
  (150 shorter events, 111.2 us)
Async XLA Ops:
  19.7 45.1 %collective-permute-start.18 = (bf16[4,256,512]{2,1,0:T(8,128)(2,1)}, bf16[4,256,512]{2,1,0:T(8,128)(2,1)}, u32[]{:S(2)}, u32[]{:S(2)}) collective-permute-start(bf16[4,256,512]{2,1,0:T(8,128)(2,1)} %bitcast.78), channel_id=1, source_target_pairs={{0,4},{4,0},{8,12},{12,8},{16,20},{20,16},{24,28},{28,24},{1,5},{5... | collective-permute-start | bytes 3145736 | tf_op jit(solution)/shard_map/ppermute | solution.py:22
  21.2 25.0 %collective-permute-start.2 = (bf16[128,256]{1,0:T(8,128)(2,1)S(1)}, bf16[128,256]{1,0:T(8,128)(2,1)S(1)}, u32[]{:S(2)}, u32[]{:S(2)}) collective-permute-start(bf16[128,256]{1,0:T(8,128)(2,1)S(1)} %maximum_convert_fusion), channel_id=1, source_target_pairs={{0,4},{4,0},{8,12},{12,8},{16,20},{20,16},{24,28},{28,24},{1,5},{5... | collective-permute-start | bytes 196616 | tf_op jit(solution)/shard_map/ppermute | solution.py:22
  54.9 25.7 %collective-permute-start.5 = (bf16[4,256,512]{2,1,0:T(8,128)(2,1)S(1)}, bf16[4,256,512]{2,1,0:T(8,128)(2,1)}, u32[]{:S(2)}, u32[]{:S(2)}) collective-permute-start(bf16[4,256,512]{2,1,0:T(8,128)(2,1)S(1)} %bitcast.77), channel_id=1, source_target_pairs={{0,4},{4,0},{8,12},{12,8},{16,20},{20,16},{24,28},{28,24},{1,5},{5... | collective-permute-start | bytes 3145736 | tf_op jit(solution)/shard_map/ppermute | solution.py:22
  66.6 20.5 %collective-permute-start.19 = (bf16[512,512]{1,0:T(8,128)(2,1)S(1)}, bf16[512,512]{1,0:T(8,128)(2,1)S(1)}, u32[]{:S(2)}, u32[]{:S(2)}) collective-permute-start(bf16[512,512]{1,0:T(8,128)(2,1)S(1)} %convolution_convert_fusion.1), channel_id=1, source_target_pairs={{0,8},{4,12},{1,9},{5,13},{2,10},{6,14},{3,11},{7,15}} | collective-permute-start | bytes 1572872 | tf_op jit(solution)/shard_map/ppermute | solution.py:428
  70.7 18.2 %collective-permute-start.22 = (bf16[512,512]{1,0:T(8,128)(2,1)S(1)}, bf16[512,512]{1,0:T(8,128)(2,1)S(1)}, u32[]{:S(2)}, u32[]{:S(2)}) collective-permute-start(bf16[512,512]{1,0:T(8,128)(2,1)S(1)} %convolution_convert_fusion), channel_id=1, source_target_pairs={{24,16},{28,20},{25,17},{29,21},{26,18},{30,22},{27,19},{31,23}} | collective-permute-start | bytes 1572872 | tf_op jit(solution)/shard_map/ppermute | solution.py:428
  87.6 21.9 %collective-permute-start.20 = (bf16[512,512]{1,0:T(8,128)(2,1)S(1)}, bf16[512,512]{1,0:T(8,128)(2,1)S(1)}, u32[]{:S(2)}, u32[]{:S(2)}) collective-permute-start(bf16[512,512]{1,0:T(8,128)(2,1)S(1)} %fusion.13), channel_id=1, source_target_pairs={{0,8},{4,12},{8,16},{12,20},{1,9},{5,13},{9,17},{13,21},{2,10},{6,... | collective-permute-start | bytes 1572872 | tf_op jit(solution)/shard_map/ppermute | solution.py:428
  89.4 25.7 %collective-permute-start.23 = (bf16[512,512]{1,0:T(8,128)(2,1)S(1)}, bf16[512,512]{1,0:T(8,128)(2,1)S(1)}, u32[]{:S(2)}, u32[]{:S(2)}) collective-permute-start(bf16[512,512]{1,0:T(8,128)(2,1)S(1)} %fusion.15), channel_id=1, source_target_pairs={{16,8},{20,12},{24,16},{28,20},{17,9},{21,13},{25,17},{29,21},{18,... | collective-permute-start | bytes 1572872 | tf_op jit(solution)/shard_map/ppermute | solution.py:428
  98.7 22.0 %collective-permute-start.7 = (bf16[512,512]{1,0:T(8,128)(2,1)S(1)}, bf16[512,512]{1,0:T(8,128)(2,1)S(1)}, u32[]{:S(2)}, u32[]{:S(2)}) collective-permute-start(bf16[512,512]{1,0:T(8,128)(2,1)S(1)} %fusion.8), channel_id=1, source_target_pairs={{0,8},{4,12},{8,16},{12,20},{1,9},{5,13},{9,17},{13,21},{2,10},{6,... | collective-permute-start | bytes 1572872 | tf_op jit(solution)/shard_map/ppermute | solution.py:428
  103.6 23.6 %collective-permute-start.10 = (bf16[512,512]{1,0:T(8,128)(2,1)S(1)}, bf16[512,512]{1,0:T(8,128)(2,1)S(1)}, u32[]{:S(2)}, u32[]{:S(2)}) collective-permute-start(bf16[512,512]{1,0:T(8,128)(2,1)S(1)} %fusion.10), channel_id=1, source_target_pairs={{16,8},{20,12},{24,16},{28,20},{17,9},{21,13},{25,17},{29,21},{18,... | collective-permute-start | bytes 1572872 | tf_op jit(solution)/shard_map/ppermute | solution.py:428
  109.9 26.9 %collective-permute-start.21 = (bf16[512,512]{1,0:T(8,128)(2,1)S(1)}, bf16[512,512]{1,0:T(8,128)(2,1)}, u32[]{:S(2)}, u32[]{:S(2)}) collective-permute-start(bf16[512,512]{1,0:T(8,128)(2,1)S(1)} %fusion.12), channel_id=1, source_target_pairs={{0,8},{4,12},{8,16},{12,20},{16,24},{20,28},{1,9},{5,13},{9,17},{1... | collective-permute-start | bytes 1572872 | tf_op jit(solution)/shard_map/ppermute | solution.py:428
  116.4 20.4 %collective-permute-start.24 = (bf16[512,512]{1,0:T(8,128)(2,1)}, bf16[512,512]{1,0:T(8,128)(2,1)}, u32[]{:S(2)}, u32[]{:S(2)}) collective-permute-start(bf16[512,512]{1,0:T(8,128)(2,1)} %fusion.14), channel_id=1, source_target_pairs={{8,0},{12,4},{16,8},{20,12},{24,16},{28,20},{9,1},{13,5},{17,9},{2... | collective-permute-start | bytes 1572872 | tf_op jit(solution)/shard_map/ppermute | solution.py:428
  121.9 23.2 %collective-permute-start.8 = (bf16[512,512]{1,0:T(8,128)(2,1)}, bf16[512,512]{1,0:T(8,128)(2,1)}, u32[]{:S(2)}, u32[]{:S(2)}) collective-permute-start(bf16[512,512]{1,0:T(8,128)(2,1)} %fusion.7), channel_id=1, source_target_pairs={{0,8},{4,12},{8,16},{12,20},{16,24},{20,28},{1,9},{5,13},{9,17},{1... | collective-permute-start | bytes 1572872 | tf_op jit(solution)/shard_map/ppermute | solution.py:428
  146.9 18.2 %collective-permute-start.12 = (bf16[512,512]{1,0:T(8,128)(2,1)S(1)}, bf16[512,512]{1,0:T(8,128)(2,1)S(1)}, u32[]{:S(2)}, u32[]{:S(2)}) collective-permute-start(bf16[512,512]{1,0:T(8,128)(2,1)S(1)} %fusion.6.refs_0_), channel_id=1, source_target_pairs={{0,8},{4,12},{8,16},{12,20},{16,24},{20,28},{1,9},{5,13},{9,17},{1... | collective-permute-start | bytes 1572872 | tf_op jit(solution)/shard_map/ppermute | solution.py:428
  151.5 20.1 %collective-permute-start.15 = (bf16[512,512]{1,0:T(8,128)(2,1)S(1)}, bf16[512,512]{1,0:T(8,128)(2,1)S(1)}, u32[]{:S(2)}, u32[]{:S(2)}) collective-permute-start(bf16[512,512]{1,0:T(8,128)(2,1)S(1)} %fusion.6.refs_0_), channel_id=1, source_target_pairs={{8,0},{12,4},{16,8},{20,12},{24,16},{28,20},{9,1},{13,5},{17,9},{2... | collective-permute-start | bytes 1572872 | tf_op jit(solution)/shard_map/ppermute | solution.py:428
  156.1 25.1 %collective-permute-start.26 = (bf16[512,512]{1,0:T(8,128)(2,1)S(1)}, bf16[512,512]{1,0:T(8,128)(2,1)S(1)}, u32[]{:S(2)}, u32[]{:S(2)}) collective-permute-start(bf16[512,512]{1,0:T(8,128)(2,1)S(1)} %collective-permute-done.25.refs_1_), channel_id=1, source_target_pairs={{8,16},{12,20},{16,24},{20,28},{9,17},{13,21},{17,25},{21,29},{10,... | collective-permute-start | bytes 1572872 | tf_op jit(solution)/shard_map/ppermute | solution.py:428
  160.3 22.5 %collective-permute-start.29 = (bf16[512,512]{1,0:T(8,128)(2,1)S(1)}, bf16[512,512]{1,0:T(8,128)(2,1)S(1)}, u32[]{:S(2)}, u32[]{:S(2)}) collective-permute-start(bf16[512,512]{1,0:T(8,128)(2,1)S(1)} %collective-permute-done.28.refs_2_), channel_id=1, source_target_pairs={{8,0},{12,4},{16,8},{20,12},{9,1},{13,5},{17,9},{21,13},{10,2},{14... | collective-permute-start | bytes 1572872 | tf_op jit(solution)/shard_map/ppermute | solution.py:428
  165.1 21.0 %collective-permute-start.13 = (bf16[512,512]{1,0:T(8,128)(2,1)S(1)}, bf16[512,512]{1,0:T(8,128)(2,1)S(1)}, u32[]{:S(2)}, u32[]{:S(2)}) collective-permute-start(bf16[512,512]{1,0:T(8,128)(2,1)S(1)} %collective-permute-done.12.refs_1_), channel_id=1, source_target_pairs={{8,16},{12,20},{16,24},{20,28},{9,17},{13,21},{17,25},{21,29},{10,... | collective-permute-start | bytes 1572872 | tf_op jit(solution)/shard_map/ppermute | solution.py:428
  171.5 22.5 %collective-permute-start.16 = (bf16[512,512]{1,0:T(8,128)(2,1)S(1)}, bf16[512,512]{1,0:T(8,128)(2,1)S(1)}, u32[]{:S(2)}, u32[]{:S(2)}) collective-permute-start(bf16[512,512]{1,0:T(8,128)(2,1)S(1)} %collective-permute-done.15.refs_2_), channel_id=1, source_target_pairs={{8,0},{12,4},{16,8},{20,12},{9,1},{13,5},{17,9},{21,13},{10,2},{14... | collective-permute-start | bytes 1572872 | tf_op jit(solution)/shard_map/ppermute | solution.py:428
  176.2 19.3 %collective-permute-start.35 = (bf16[2,256,512]{2,1,0:T(8,128)(2,1)S(1)}, bf16[2,256,512]{2,1,0:T(8,128)(2,1)S(1)}, u32[]{:S(2)}, u32[]{:S(2)}) collective-permute-start(bf16[2,256,512]{2,1,0:T(8,128)(2,1)S(1)} %get-tuple-element.43), channel_id=1, source_target_pairs={{0,4},{4,0},{8,12},{12,8},{16,20},{20,16},{24,28},{28,24},{1,5},{5... | collective-permute-start | bytes 1572872 | tf_op jit(solution)/shard_map/ppermute | solution.py:22
  181.2 18.6 %collective-permute-start.27 = (bf16[512,512]{1,0:T(8,128)(2,1)S(1)}, bf16[512,512]{1,0:T(8,128)(2,1)S(1)}, u32[]{:S(2)}, u32[]{:S(2)}) collective-permute-start(bf16[512,512]{1,0:T(8,128)(2,1)S(1)} %collective-permute-done.26.refs_1_), channel_id=1, source_target_pairs={{16,24},{20,28},{17,25},{21,29},{18,26},{22,30},{19,27},{23,31}} | collective-permute-start | bytes 1572872 | tf_op jit(solution)/shard_map/ppermute | solution.py:428
  182.8 22.5 %collective-permute-start.30 = (bf16[512,512]{1,0:T(8,128)(2,1)S(1)}, bf16[512,512]{1,0:T(8,128)(2,1)S(1)}, u32[]{:S(2)}, u32[]{:S(2)}) collective-permute-start(bf16[512,512]{1,0:T(8,128)(2,1)S(1)} %collective-permute-done.29.refs_2_), channel_id=1, source_target_pairs={{8,0},{12,4},{9,1},{13,5},{10,2},{14,6},{11,3},{15,7}} | collective-permute-start | bytes 1572872 | tf_op jit(solution)/shard_map/ppermute | solution.py:428
  194.0 18.2 %collective-permute-start.32 = (bf16[2,256,512]{2,1,0:T(8,128)(2,1)S(1)}, bf16[2,256,512]{2,1,0:T(8,128)(2,1)S(1)}, u32[]{:S(2)}, u32[]{:S(2)}) collective-permute-start(bf16[2,256,512]{2,1,0:T(8,128)(2,1)S(1)} %get-tuple-element.40), channel_id=1, source_target_pairs={{0,4},{4,0},{8,12},{12,8},{16,20},{20,16},{24,28},{28,24},{1,5},{5... | collective-permute-start | bytes 1572872 | tf_op jit(solution)/shard_map/ppermute | solution.py:22
  195.5 21.6 %collective-permute-start.14 = (bf16[512,512]{1,0:T(8,128)(2,1)S(1)}, bf16[512,512]{1,0:T(8,128)(2,1)S(1)}, u32[]{:S(2)}, u32[]{:S(2)}) collective-permute-start(bf16[512,512]{1,0:T(8,128)(2,1)S(1)} %collective-permute-done.13.refs_1_), channel_id=1, source_target_pairs={{16,24},{20,28},{17,25},{21,29},{18,26},{22,30},{19,27},{23,31}} | collective-permute-start | bytes 1572872 | tf_op jit(solution)/shard_map/ppermute | solution.py:428
  196.2 20.9 %collective-permute-start.17 = (bf16[512,512]{1,0:T(8,128)(2,1)S(1)}, bf16[512,512]{1,0:T(8,128)(2,1)S(1)}, u32[]{:S(2)}, u32[]{:S(2)}) collective-permute-start(bf16[512,512]{1,0:T(8,128)(2,1)S(1)} %collective-permute-done.16.refs_2_), channel_id=1, source_target_pairs={{8,0},{12,4},{9,1},{13,5},{10,2},{14,6},{11,3},{15,7}} | collective-permute-start | bytes 1572872 | tf_op jit(solution)/shard_map/ppermute | solution.py:428
  (35 other events, 403.5 us)

commit v2 on v1

--- a/solution.py
+++ b/solution.py
@@ -108,81 +108,87 @@
     )(table, weight)
 
 
-def place_kernel(starts, table, *refs):
-    out = refs[-1]
-    part = out.shape[2]
-    step = pl.program_id(0)
-    for j in range(len(starts) - 1):
-
-        @pl.when((step >= starts[j]) & (step < starts[j + 1]))
-        def _(ref=refs[j]):
-            for layer in range(out.shape[1]):
-                out[:, layer, :] = ref[0, :, layer * part : (layer + 1) * part]
-
-
-def place(groups, table, at, shape, held):
-    feats, layers, _ = shape
-    cols = groups[0].shape[2]
-    part = cols // layers
-    starts = [0]
-    for g in groups:
-        starts.append(starts[-1] + g.shape[0])
-
-    def spec(j):
-        most = groups[j].shape[0] - 1
-
-        def index(i, t):
-            return (jnp.clip(i - starts[j], 0, most), 0, 0)
-
-        return pl.BlockSpec((1, feats, cols), index)
-
-    specs = [spec(j) for j in range(len(groups))]
-    operands = list(groups)
-    aliases = {}
-    if held is not None:
-        specs.append(pl.BlockSpec(memory_space=pl.ANY))
-        operands.append(held)
-        aliases = {len(operands): 0}
-    return pl.pallas_call(
-        functools.partial(place_kernel, starts),
+def place_kernel(count, at, sizes, table, *refs):
+    groups, out, sems = refs[:count], refs[-2], refs[-1]
+    part = groups[0].shape[3]
+    copies = []
+    for j, size in enumerate(sizes):
+        for i in range(size):
+            entry = at + 2 * len(copies)
+            start = pl.multiple_of(table[entry] * part, part)
+            copy = pltpu.make_async_copy(
+                groups[j].at[i], out.at[:, :, pl.ds(start, part)], sems.at[len(copies)]
+            )
+            copies.append((copy, table[entry + 1] == 1))
+    for copy, valid in copies:
+
+        @pl.when(valid)
+        def _(copy=copy):
+            copy.start()
+
+    for copy, valid in copies:
+
+        @pl.when(valid)
+        def _(copy=copy):
+            copy.wait()
+
+
+def place(groups, table, at, held):
+    sizes = [g.shape[0] for g in groups]
+    body = functools.partial(place_kernel, len(groups), at, sizes)
+    return pl.pallas_call(
+        body,
         grid_spec=pltpu.PrefetchScalarGridSpec(
             num_scalar_prefetch=1,
-            grid=(starts[-1],),
-            in_specs=specs,
+            grid=(1,),
+            in_specs=[pl.BlockSpec(g.shape, lambda i, t: (0, 0, 0, 0)) for g in groups]
+            + [pl.BlockSpec(memory_space=pl.ANY)],
+            out_specs=pl.BlockSpec(memory_space=pl.ANY),
+            scratch_shapes=[pltpu.SemaphoreType.DMA((sum(sizes),))],
+        ),
+        out_shape=jax.ShapeDtypeStruct(held.shape, held.dtype),
+        input_output_aliases={len(groups) + 1: 0},
+        compiler_params=limits(16),
+        cost_estimate=cost(0, 4 * sum(g.size for g in groups)),
+    )(table, *groups, held)
+
+
+def goal_kernel(ends, units, at, table, resid, bias, out):
+    layers = resid.shape[1]
+    part = resid.shape[2] // units
+    for e in range(ends):
+        entry = at + 1 + e
+        here = pl.ds(pl.multiple_of(table[entry] * part, part), part)
+        for layer in range(layers):
+            rows = resid[:, layer, here].astype(F32)
+            out[0, e, :, layer * part : (layer + 1) * part] = (
+                bias[layer, here][None, :] - rows
+            )
+
+
+def goals_of(resid, bias, table, at, chains, ends, units, part):
+    tokens, layers, _ = resid.shape
+    wide = units // 2 * part
+
+    def block(i, t):
+        return t[at] + 2 * i
+
+    return pl.pallas_call(
+        functools.partial(goal_kernel, ends, units // 2, at),
+        grid_spec=pltpu.PrefetchScalarGridSpec(
+            num_scalar_prefetch=1,
+            grid=(chains,),
+            in_specs=[
+                pl.BlockSpec((tokens, layers, wide), lambda i, t: (0, 0, block(i, t))),
+                pl.BlockSpec((layers, wide), lambda i, t: (0, block(i, t))),
+            ],
             out_specs=pl.BlockSpec(
-                (feats, layers, part), lambda i, t: (0, 0, t[at + i])
+                (1, ends, tokens, layers * part), lambda i, t: (i, 0, 0, 0)
             ),
         ),
-        out_shape=jax.ShapeDtypeStruct(shape, BF16),
-        input_output_aliases=aliases,
-        compiler_params=limits(16),
-        cost_estimate=cost(0, 4 * starts[-1] * feats * cols),
-    )(table, *operands)
-
-
-def goal_kernel(table, resid, bias, out):
-    part = resid.shape[2]
-    for layer in range(resid.shape[1]):
-        rows = resid[:, layer, :].astype(F32)
-        out[0, :, layer * part : (layer + 1) * part] = bias[layer][None, :] - rows
-
-
-def goals_of(resid, bias, table, at, count, part):
-    tokens, layers, _ = resid.shape
-    return pl.pallas_call(
-        goal_kernel,
-        grid_spec=pltpu.PrefetchScalarGridSpec(
-            num_scalar_prefetch=1,
-            grid=(count,),
-            in_specs=[
-                pl.BlockSpec((tokens, layers, part), lambda i, t: (0, 0, t[at + i])),
-                pl.BlockSpec((layers, part), lambda i, t: (0, t[at + i])),
-            ],
-            out_specs=pl.BlockSpec((1, tokens, layers * part), lambda i, t: (i, 0, 0)),
-        ),
-        out_shape=jax.ShapeDtypeStruct((count, tokens, layers * part), F32),
-        compiler_params=limits(12),
-        cost_estimate=cost(0, 6 * count * tokens * layers * part),
+        out_shape=jax.ShapeDtypeStruct((chains, ends, tokens, layers * part), F32),
+        compiler_params=limits(24),
+        cost_estimate=cost(0, 6 * chains * ends * tokens * layers * part),
     )(table, resid, bias)
 
 
@@ -226,8 +232,9 @@
     feats, layers, part = near.shape
     grad = (dot(act_t[...], e, ((1,), (0,))) * scale).astype(BF16)
     for layer in range(layers):
-        near[:, layer, :] = grad[:feats, layer * part : (layer + 1) * part]
-    far[0] = grad[feats:]
+        columns = slice(layer * part, (layer + 1) * part)
+        near[:, layer, :] = grad[:feats, columns]
+        far[0, :, layer, :] = grad[feats:, columns]
     more = dot(e, weights[0], ((1,), (1,))) * valid.astype(F32)
 
     @pl.when(step == 0)
@@ -271,13 +278,13 @@
                 pl.BlockSpec(
                     (feats, layers, part), lambda i, t: (0, 0, t[at + 4 * i + 3])
                 ),
-                pl.BlockSpec((1, feats, cols), lambda i, t: (i, 0, 0)),
+                pl.BlockSpec((1, feats, layers, part), lambda i, t: (i, 0, 0, 0)),
                 pl.BlockSpec((tokens, double), lambda i, t: (0, 0)),
             ],
         ),
         out_shape=[
             jax.ShapeDtypeStruct(shape, BF16),
-            jax.ShapeDtypeStruct((m, feats, cols), BF16),
+            jax.ShapeDtypeStruct((m, feats, layers, part), BF16),
             jax.ShapeDtypeStruct((tokens, double), F32),
         ],
         input_output_aliases=aliases,
@@ -289,9 +296,13 @@
 
 
 def groups_of(units, steps):
-    groups = [[(0, 0)]]
+    several = 1 if units == steps + 1 else 2
+    groups, now = [[(0, 0)]], []
     for s in range(1, steps + 1):
-        groups.append([(s, -1), (s, 1)] if 2 * s < units else [(s, 0)])
+        now += [(s, -1), (s, 1)] if 2 * s < units else [(s, 0)]
+        if s % several == 0 or s == steps:
+            groups.append(now)
+            now = []
     return groups
 
 
@@ -337,14 +348,10 @@
             [of * chains + k for of in (1 - side, side) for k in range(1, chains)],
         )
         sign = -1 if pos < line // 2 else 1
-        add(
-            "goals",
-            [
-                (side * chains + k) * units + centre + sign * e
-                for k in range(chains)
-                for e in range(ends)
-            ],
-        )
+        block = int(pos >= line // 2)
+        add("goals", [2 * side * chains + block])
+        add("goals_at", [(centre + sign * e) % (units // 2) for e in range(ends)])
+        add("edges", [int(pos in (0, line - 1))] * chains * ends)
         for k in range(chains):
             base = (side * chains + k) * units
             for i, group in enumerate(groups):
@@ -354,19 +361,19 @@
                     way, unit, valid = taken(s, d)
                     src = 0
                     if way:
-                        src = 1 + 2 * sorted({e[0] for e in came}).index(s) + (way > 0)
+                        src = 1 + 2 * sorted({e[0] for e in came}).index(s)
+                        src += int((way < 0) == (pos % 2 == 0))
                     values += [src, unit, valid, base + unit]
                 add(f"use_{k}_{i}", values)
-        far = [
-            [
-                [((1 - side) * chains + k) * units + taken(s, d)[1] for s, d in group]
-                for group in groups
-            ]
-            for k in range(chains)
-        ]
         for k in range(chains):
-            add(f"far_{k}", sum(far[k][:-1], []))
-        add("far_last", sum((far[k][-1] for k in range(chains)), []))
+            base = ((1 - side) * chains + k) * units
+            values = []
+            for s, d in sum(groups, []):
+                _, unit, valid = taken(s, d)
+                if d and not 0 <= centre + d * s < units:
+                    valid = 0
+                values += [base + unit, valid]
+            add(f"far_{k}", values)
         rows.append(row)
     return np.array(rows, np.int32), at
 
@@ -416,16 +423,26 @@
     for b in reversed(range(bits)):
         come = swap(act, "cuts", b)
         act = joined(act, come, ups[b])
-    goals = goals_of(resid, dec_bias, table, at["goals"], chains * ends, part)
-
-    def shift(value, step, sources):
+    goals = goals_of(
+        resid, dec_bias, table, at["goals"], chains, ends, units, part
+    )
+
+    def exchange(value, ups, downs, even):
         pairs = [
-            (2 * i + s, 2 * (i + step) + s)
-            for i in sources
-            if 0 <= i < line and 0 <= i + step < line
+            (2 * i + s, 2 * j + s)
+            for i in range(line)
+            for j, sources in ((i + 1, ups), (i - 1, downs))
+            if i in sources and 0 <= j < line and (i % 2 == 0) == (even == (j > i))
             for s in range(2)
         ]
+        if not pairs:
+            return None
         return lax.ppermute(value, "layer", pairs)
+
+    def plus(value, more):
+        return value if more is None else value + more.astype(F32)
+
+    even = pos % 2 == 0
 
     both = [
         lax.optimization_barrier(jnp.concatenate([own[k], got[k]], 1))
@@ -439,51 +456,52 @@
     def recon(k, u):
         return dot(act, weights(k, u), ((1,), (0,)))
 
-    right, left = [None] * chains, [None] * chains
+    ahead, behind = [None] * chains, [None] * chains
     errs = [[None] * ends for _ in range(chains)]
     for s in range(1, steps + 1):
+        up, down = units - s + pos, s - line + pos
+        one = jnp.clip(jnp.where(even, up, down), 0, units - 1)
+        two = jnp.clip(jnp.where(even, down, up), 0, units - 1)
+        ways = range(0, s), range(line - s, line)
         for k in range(chains):
-            r = recon(k, jnp.clip(units - s + pos, 0, units - 1))
-            l = recon(k, jnp.clip(s - line + pos, 0, units - 1))
+            give = plus(recon(k, one), behind[k]).astype(BF16)
+            first = exchange(give, *ways, True)
+            behind_next = None
             if s > 1:
-                r = r + right[k].astype(F32)
-                l = l + left[k].astype(F32)
-            right[k] = shift(r.astype(BF16), 1, range(0, s))
-            left[k] = shift(l.astype(BF16), -1, range(line - s, line))
+                give = plus(recon(k, two), ahead[k]).astype(BF16)
+                behind_next = exchange(give, *ways, False)
+            ahead[k], behind[k] = first, behind_next
             late = steps - s
             if late < ends:
                 u = jnp.where(pos < line // 2, centre - late, centre + late)
-                err = recon(k, u) + right[k].astype(F32) + left[k].astype(F32)
-                err = err + goals[k * ends + late]
+                err = plus(plus(recon(k, u), ahead[k]), behind[k])
+                err = err + goals[k, late]
                 errs[k][late] = err.astype(BF16)
 
     dact = dec_grad = None
     fars = [[] for _ in range(chains)]
     groups = groups_of(units, steps)
-    right = [errs[k][0] for k in range(chains)]
-    left = [errs[k][0] for k in range(chains)]
+    ahead = [errs[k][0] for k in range(chains)]
+    behind = [errs[k][0] for k in range(chains)]
     came = [[] for _ in range(chains)]
 
     def put(name, which, dec_grad):
-        return place(which, table, at[name], dec_weight.shape, dec_grad)
+        return place(which, table, at[name], dec_grad)
 
     for s in range(steps + 1):
+        ways = range(max(s - ends, 0), line - 1), range(1, line + min(ends - s, 0))
         for k in range(chains if s else 0):
-            right[k] = shift(right[k], 1, range(max(s - ends, 0), line - 1))
-            left[k] = shift(
-                left[k], -1, range(1, min(line - 1 + ends - s, line - 1) + 1)
-            )
-            if s < ends:
-                right[k] = jnp.where(pos == 0, errs[k][s], right[k])
-                left[k] = jnp.where(pos == line - 1, errs[k][s], left[k])
-            came[k] += [right[k], left[k]]
+            first = exchange(behind[k], *ways, True)
+            second = exchange(ahead[k], *ways, False)
+            if 0 < s < ends:
+                edge = table[at["edges"] + k * ends + s].astype(BF16)
+                second = second + errs[k][s] * edge
+            ahead[k], behind[k] = first, second
+            came[k] += [first, first if second is None else second]
         for k in range(chains):
             for i, group in enumerate(groups):
                 if group[-1][0] != s:
                     continue
-                if i == len(groups) - 1 and k == chains - 1:
-                    for c in range(chains):
-                        dec_grad = put(f"far_{c}", fars[c][:i], dec_grad)
                 dec_grad, far, dact = use_of(
                     act_t,
                     both[k],
@@ -498,7 +516,8 @@
                 )
                 came[k] = []
                 fars[k].append(swap(far, "layer", 0))
-    dec_grad = put("far_last", [f[-1] for f in fars], dec_grad)
+    for k in range(chains):
+        dec_grad = put(f"far_{k}", fars[k], dec_grad)
 
     flats = []
     for i in range(FLATS):

time: 252 us -> 288 us (1.14)
  waiting for transfers between devices: 91.7 us -> 150 us
  starting transfers between devices: 69.6 us -> 50.6 us
  Pallas kernels: 49.9 us -> 46.9 us
    ppermute x24 -> x20, waiting for transfers between devices: 38.8 us -> 68.1 us  [exchange(): return lax.ppermute(value, 'layer', pairs)]
    ppermute x20, waiting for transfers between devices: 53 us -> 82.3 us  [swap(): return lax.ppermute(value, axis, [(i, i ^ 1 << bit) for i in range(size)])]
    ppermute x24 -> x20, starting transfers between devices: 48.9 us -> 34.8 us  [exchange(): return lax.ppermute(value, 'layer', pairs)]
    pallas_call x4 -> x3, Pallas kernels: 11.5 us -> 5.48 us  [the longest x2 3.1 us: place(): pl.pallas_call(body, grid_spec=pltpu.PrefetchScalarGridSpec(num_scalar_pr...]
    ppermute x20, starting transfers between devices: 20.7 us -> 15.8 us  [swap(): return lax.ppermute(value, axis, [(i, i ^ 1 << bit) for i in range(size)])]
    dot_general x15 -> x13, matrix products: 21.1 us -> 19.7 us  [dot(): return lax.dot_general(a, b, (dims, ((), ())), preferred_element_type=F32)]
  transfers between devices with their start and end apart: 44 -> 40, of which waited for: 19 -> 22; matrix products, arithmetic and copies ran while one was open for 6% -> 5% of each run, Pallas kernels for 17% -> 14%
where the time goes in v2:
time: 288 us; the launch traced here: 287 us
  waiting for transfers between devices  150 us (52%)
  starting transfers between devices  50.6 us (18%)
  Pallas kernels  46.9 us (16%)
  matrix products  19.7 us (7%)
  local copies, waits for them, and re-layouts  14.1 us (5%)
  other arithmetic  3.86 us (1%)
    ppermute x20, waiting for transfers between devices, swap(): return lax.ppermute(value, axis, [(i, i ^ 1 << bit) for i in range(size)])  82.3 us
    ppermute x20, waiting for transfers between devices, exchange(): return lax.ppermute(value, 'layer', pairs)  68.1 us
    ppermute x20, starting transfers between devices, exchange(): return lax.ppermute(value, 'layer', pairs)  34.8 us
    pallas_call x8, Pallas kernels, use_of(): pl.pallas_call(body, grid_spec=pltpu.PrefetchScalarGridSpec(num_scalar_pr...  20.8 us
    dot_general x13, matrix products, dot(): return lax.dot_general(a, b, (dims, ((), ())), preferred_element_type=F32)  19.7 us
    ppermute x20, starting transfers between devices, swap(): return lax.ppermute(value, axis, [(i, i ^ 1 << bit) for i in range(size)])  15.8 us
    unnamed x30, local copies, waits for them, and re-layouts  12.9 us
    pallas_call x4, Pallas kernels, prep(): pl.pallas_call(prep_kernel, grid_spec=pltpu.PrefetchScalarGridSpec(num_sc...  8.67 us
  transfers between devices with their start and end apart: 40, of which 22 were waited for; matrix products, arithmetic and copies ran while one was open for 5% of the time, Pallas kernels for 14%

profile of v2, /device:TPU:0, one launch (start us, length us, event | category | flops | bytes accessed | tf_op | source)
XLA Modules:
  0.0 286.8 jit_solution(1335040164335165049)
XLA Ops:
  0.6 9.3 %fusion.14 = f32[512,256]{1,0:T(8,128)S(1)} fusion(bf16[2,4096,256]{2,1,0:T(8,128)(2,1)} %param.7, bf16[512,2,4096]{2,1,0:T(2,128)(2,1)} %resid.1), kind=kOutput, calls=%fused_computation.28 | convolution fusion | flops 2147483648 | bytes 13107200 | tf_op jit(solution)/shard_map/dot_general | solution.py:40
  15.9 3.8 %shard_map.86 = bf16[1,4,256,512]{3,2,1,0:T(8,128)(2,1)} custom-call(s32[68]{0:T(128)} %fusion.56.table, bf16[256,2,4096]{2,1,0:T(2,128)(2,1)} %rows.15), custom_call_target="tpu_custom_call" | custom-call | bytes 2097152 | tf_op jit(solution)/shard_map/pallas_call | solution.py:95
  21.8 24.4 %collective-permute-done.2 = bf16[128,256]{1,0:T(8,128)(2,1)S(1)} collective-permute-done((bf16[128,256]{1,0:T(8,128)(2,1)S(1)}, bf16[128,256]{1,0:T(8,128)(2,1)S(1)}, u32[]{:S(2)}, u32[]{:S(2)}) %collective-permute-start.2) | collective-permute-done | bytes 65568 | tf_op jit(solution)/shard_map/ppermute | solution.py:22
  46.6 4.7 %collective-permute-done.3 = bf16[128,512]{1,0:T(8,128)(2,1)S(1)} collective-permute-done((bf16[128,512]{1,0:T(8,128)(2,1)S(1)}, bf16[128,512]{1,0:T(8,128)(2,1)S(1)}, u32[]{:S(2)}, u32[]{:S(2)}) %collective-permute-start.3) | collective-permute-done | bytes 131104 | tf_op jit(solution)/shard_map/ppermute | solution.py:22
  75.1 6.7 %collective-permute-done.5 = bf16[4,256,512]{2,1,0:T(8,128)(2,1)} collective-permute-done((bf16[4,256,512]{2,1,0:T(8,128)(2,1)}, bf16[4,256,512]{2,1,0:T(8,128)(2,1)}, u32[]{:S(2)}, u32[]{:S(2)}) %collective-permute-start.5) | collective-permute-done | bytes 1048608 | tf_op jit(solution)/shard_map/ppermute | solution.py:22
  90.1 6.7 %collective-permute-done.18 = bf16[512,512]{1,0:T(8,128)(2,1)S(1)} collective-permute-done((bf16[512,512]{1,0:T(8,128)(2,1)S(1)}, bf16[512,512]{1,0:T(8,128)(2,1)S(1)}, u32[]{:S(2)}, u32[]{:S(2)}) %collective-permute-start.18) | collective-permute-done | bytes 524320 | tf_op jit(solution)/shard_map/ppermute | solution.py:440
  98.7 9.3 %collective-permute-done.6 = bf16[512,512]{1,0:T(8,128)(2,1)S(1)} collective-permute-done((bf16[512,512]{1,0:T(8,128)(2,1)S(1)}, bf16[512,512]{1,0:T(8,128)(2,1)S(1)}, u32[]{:S(2)}, u32[]{:S(2)}) %collective-permute-start.6) | collective-permute-done | bytes 524320 | tf_op jit(solution)/shard_map/ppermute | solution.py:440
  110.6 5.3 %collective-permute-start.17 = (bf16[512,512]{1,0:T(8,128)(2,1)}, bf16[512,512]{1,0:T(8,128)(2,1)}, u32[]{:S(2)}, u32[]{:S(2)}) collective-permute-start(bf16[512,512]{1,0:T(8,128)(2,1)} %fusion.11), channel_id=1, source_target_pairs={{0,8},{4,12},{8,0},{12,4},{16,24},{20,28},{24,16},{28,20},{1,9},{5... | collective-permute-start | bytes 1572872 | tf_op jit(solution)/shard_map/ppermute | solution.py:440
  123.2 4.8 %collective-permute-start.8 = (bf16[512,512]{1,0:T(8,128)(2,1)}, bf16[512,512]{1,0:T(8,128)(2,1)}, u32[]{:S(2)}, u32[]{:S(2)}) collective-permute-start(bf16[512,512]{1,0:T(8,128)(2,1)} %fusion.7), channel_id=1, source_target_pairs={{0,8},{4,12},{8,0},{12,4},{16,24},{20,28},{24,16},{28,20},{1,9},{5... | collective-permute-start | bytes 1572872 | tf_op jit(solution)/shard_map/ppermute | solution.py:440
  135.8 6.1 %collective-permute-done.8 = bf16[512,512]{1,0:T(8,128)(2,1)} collective-permute-done((bf16[512,512]{1,0:T(8,128)(2,1)}, bf16[512,512]{1,0:T(8,128)(2,1)}, u32[]{:S(2)}, u32[]{:S(2)}) %collective-permute-start.8) | collective-permute-done | bytes 524320 | tf_op jit(solution)/shard_map/ppermute | solution.py:440
  147.5 5.5 %collective-permute-done.20.refs_1_ = bf16[512,512]{1,0:T(8,128)(2,1)S(1)} collective-permute-done((bf16[512,512]{1,0:T(8,128)(2,1)S(1)}, bf16[512,512]{1,0:T(8,128)(2,1)S(1)}, u32[]{:S(2)}, u32[]{:S(2)}) %collective-permute-start.20) | collective-permute-done | bytes 524320 | tf_op jit(solution)/shard_map/ppermute | solution.py:440
  153.7 9.8 %collective-permute-done.11.refs_1_ = bf16[512,512]{1,0:T(8,128)(2,1)S(1)} collective-permute-done((bf16[512,512]{1,0:T(8,128)(2,1)S(1)}, bf16[512,512]{1,0:T(8,128)(2,1)S(1)}, u32[]{:S(2)}, u32[]{:S(2)}) %collective-permute-start.11) | collective-permute-done | bytes 524320 | tf_op jit(solution)/shard_map/ppermute | solution.py:440
  173.7 3.9 %shard_map.89 = (bf16[256,2,4096]{2,1,0:T(2,128)(2,1)}, bf16[2,256,2,256]{3,2,1,0:T(2,128)(2,1)S(1)}, f32[512,512]{1,0:T(8,128)S(1)}) custom-call(s32[68]{0:T(128)S(1)} %copy-done.9, bf16[512,512]{1,0:T(8,128)(2,1)S(1)} %shard_map.81.act_t, bf16[4,512,512]{2,1,0:T(8,128)(2,1)S(1)} %pad_maximum_fusion.1.weights, ...), custom_call_target="tpu_custom_call", output_to_operand_aliasing={{2}: (6, {}), {0}: (7, {})} | custom-call | flops 1073741824 | bytes 3145728 | tf_op jit(solution)/shard_map/pallas_call | solution.py:271
  177.6 3.9 %shard_map.90 = (bf16[256,2,4096]{2,1,0:T(2,128)(2,1)}, bf16[2,256,2,256]{3,2,1,0:T(2,128)(2,1)S(1)}, f32[512,512]{1,0:T(8,128)S(1)}) custom-call(s32[68]{0:T(128)S(1)} %copy-done.9, bf16[512,512]{1,0:T(8,128)(2,1)S(1)} %shard_map.81.act_t, bf16[4,512,512]{2,1,0:T(8,128)(2,1)S(1)} %copy-done.2, ...), custom_call_target="tpu_custom_call", output_to_operand_aliasing={{2}: (6, {}), {0}: (7, {})} | custom-call | flops 1073741824 | bytes 3145728 | tf_op jit(solution)/shard_map/pallas_call | solution.py:271
  185.7 9.0 %collective-permute-done.24.refs_1_ = bf16[512,512]{1,0:T(8,128)(2,1)S(1)} collective-permute-done((bf16[512,512]{1,0:T(8,128)(2,1)S(1)}, bf16[512,512]{1,0:T(8,128)(2,1)S(1)}, u32[]{:S(2)}, u32[]{:S(2)}) %collective-permute-start.24) | collective-permute-done | bytes 524320 | tf_op jit(solution)/shard_map/ppermute | solution.py:440
  196.9 9.0 %collective-permute-done.22.refs_1_.refs_2_ = bf16[512,512]{1,0:T(8,128)(2,1)S(1)} collective-permute-done((bf16[512,512]{1,0:T(8,128)(2,1)S(1)}, bf16[512,512]{1,0:T(8,128)(2,1)S(1)}, u32[]{:S(2)}, u32[]{:S(2)}) %collective-permute-start.22) | collective-permute-done | bytes 524320 | tf_op jit(solution)/shard_map/ppermute | solution.py:440
  208.2 7.4 %collective-permute-done.13.refs_1_.refs_2_ = bf16[512,512]{1,0:T(8,128)(2,1)S(1)} collective-permute-done((bf16[512,512]{1,0:T(8,128)(2,1)S(1)}, bf16[512,512]{1,0:T(8,128)(2,1)S(1)}, u32[]{:S(2)}, u32[]{:S(2)}) %collective-permute-start.13) | collective-permute-done | bytes 524320 | tf_op jit(solution)/shard_map/ppermute | solution.py:440
  220.2 5.0 %collective-permute-done.28 = bf16[128,512]{1,0:T(8,128)(2,1)S(1)} collective-permute-done((bf16[128,512]{1,0:T(8,128)(2,1)S(1)}, bf16[128,512]{1,0:T(8,128)(2,1)S(1)}, u32[]{:S(2)}, u32[]{:S(2)}) %collective-permute-start.28) | collective-permute-done | bytes 131104 | tf_op jit(solution)/shard_map/ppermute | solution.py:22
  229.4 7.0 %collective-permute-done.29 = bf16[128,256]{1,0:T(8,128)(2,1)S(1)} collective-permute-done((bf16[128,256]{1,0:T(8,128)(2,1)S(1)}, bf16[128,256]{1,0:T(8,128)(2,1)S(1)}, u32[]{:S(2)}, u32[]{:S(2)}) %collective-permute-start.29) | collective-permute-done | bytes 65568 | tf_op jit(solution)/shard_map/ppermute | solution.py:22
  236.4 5.6 %collective-permute-done.36.refs_0_ = bf16[1,256,2,256]{3,2,1,0:T(2,128)(2,1)S(1)} collective-permute-done((bf16[1,256,2,256]{3,2,1,0:T(2,128)(2,1)S(1)}, bf16[1,256,2,256]{3,2,1,0:T(2,128)(2,1)S(1)}, u32[]{:S(2)}, u32[]{:S(2)}) %collective-permute-start.36) | collective-permute-done | bytes 262176 | tf_op jit(solution)/shard_map/ppermute | solution.py:22
  243.5 15.3 %collective-permute-done.38.refs_2_ = bf16[1,256,2,256]{3,2,1,0:T(2,128)(2,1)S(1)} collective-permute-done((bf16[1,256,2,256]{3,2,1,0:T(2,128)(2,1)S(1)}, bf16[1,256,2,256]{3,2,1,0:T(2,128)(2,1)S(1)}, u32[]{:S(2)}, u32[]{:S(2)}) %collective-permute-start.38) | collective-permute-done | bytes 262176 | tf_op jit(solution)/shard_map/ppermute | solution.py:22
  260.9 3.6 %collective-permute-done.39.refs_3_ = bf16[1,256,2,256]{3,2,1,0:T(2,128)(2,1)S(1)} collective-permute-done((bf16[1,256,2,256]{3,2,1,0:T(2,128)(2,1)S(1)}, bf16[1,256,2,256]{3,2,1,0:T(2,128)(2,1)S(1)}, u32[]{:S(2)}, u32[]{:S(2)}) %collective-permute-start.39) | collective-permute-done | bytes 262176 | tf_op jit(solution)/shard_map/ppermute | solution.py:22
  275.7 4.5 %collective-permute-done.35.refs_3_ = bf16[1,256,2,256]{3,2,1,0:T(2,128)(2,1)S(1)} collective-permute-done((bf16[1,256,2,256]{3,2,1,0:T(2,128)(2,1)S(1)}, bf16[1,256,2,256]{3,2,1,0:T(2,128)(2,1)S(1)}, u32[]{:S(2)}, u32[]{:S(2)}) %collective-permute-start.35) | collective-permute-done | bytes 262176 | tf_op jit(solution)/shard_map/ppermute | solution.py:22
  281.9 4.9 %shard_map.95 = bf16[2,4096,256]{2,1,0:T(8,128)(2,1)} custom-call(bf16[2,128,4096]{2,1,0:T(8,128)(2,1)S(1)} %shard_map.77.refs_0_, bf16[2,128,4096]{2,1,0:T(8,128)(2,1)S(1)} %shard_map.78.refs_1_, bf16[2,128,4096]{2,1,0:T(8,128)(2,1)S(1)} %shard_map.79.refs_2_, bf16[2,128,4096]{2,1,0:T(8,128)(2,1)S(1)} %shard_map.80.refs_3_, ...), custom_call_target="tpu_custom_call" | custom-call | flops 2147483648 | bytes 12582912 | tf_op jit(solution)/shard_map/pallas_call | solution.py:61
  (139 shorter events, 110.2 us)
Async XLA Ops:
  19.7 46.9 %collective-permute-start.14 = (bf16[4,256,512]{2,1,0:T(8,128)(2,1)}, bf16[4,256,512]{2,1,0:T(8,128)(2,1)S(1)}, u32[]{:S(2)}, u32[]{:S(2)}) collective-permute-start(bf16[4,256,512]{2,1,0:T(8,128)(2,1)} %bitcast.69), channel_id=1, source_target_pairs={{0,4},{4,0},{8,12},{12,8},{16,20},{20,16},{24,28},{28,24},{1,5},{5... | collective-permute-start | bytes 3145736 | tf_op jit(solution)/shard_map/ppermute | solution.py:22
  21.2 25.0 %collective-permute-start.2 = (bf16[128,256]{1,0:T(8,128)(2,1)S(1)}, bf16[128,256]{1,0:T(8,128)(2,1)S(1)}, u32[]{:S(2)}, u32[]{:S(2)}) collective-permute-start(bf16[128,256]{1,0:T(8,128)(2,1)S(1)} %maximum_convert_fusion), channel_id=1, source_target_pairs={{0,4},{4,0},{8,12},{12,8},{16,20},{20,16},{24,28},{28,24},{1,5},{5... | collective-permute-start | bytes 196616 | tf_op jit(solution)/shard_map/ppermute | solution.py:22
  55.9 25.9 %collective-permute-start.5 = (bf16[4,256,512]{2,1,0:T(8,128)(2,1)}, bf16[4,256,512]{2,1,0:T(8,128)(2,1)}, u32[]{:S(2)}, u32[]{:S(2)}) collective-permute-start(bf16[4,256,512]{2,1,0:T(8,128)(2,1)} %bitcast.3), channel_id=1, source_target_pairs={{0,4},{4,0},{8,12},{12,8},{16,20},{20,16},{24,28},{28,24},{1,5},{5... | collective-permute-start | bytes 3145736 | tf_op jit(solution)/shard_map/ppermute | solution.py:22
  69.8 19.1 %collective-permute-start.15 = (bf16[512,512]{1,0:T(8,128)(2,1)S(1)}, bf16[512,512]{1,0:T(8,128)(2,1)S(1)}, u32[]{:S(2)}, u32[]{:S(2)}) collective-permute-start(bf16[512,512]{1,0:T(8,128)(2,1)S(1)} %convolution_convert_fusion.1), channel_id=1, source_target_pairs={{0,8},{4,12},{24,16},{28,20},{1,9},{5,13},{25,17},{29,21},{2,10},{... | collective-permute-start | bytes 1572872 | tf_op jit(solution)/shard_map/ppermute | solution.py:440
  73.7 23.1 %collective-permute-start.18 = (bf16[512,512]{1,0:T(8,128)(2,1)S(1)}, bf16[512,512]{1,0:T(8,128)(2,1)S(1)}, u32[]{:S(2)}, u32[]{:S(2)}) collective-permute-start(bf16[512,512]{1,0:T(8,128)(2,1)S(1)} %convolution_convert_fusion), channel_id=1, source_target_pairs={{0,8},{4,12},{24,16},{28,20},{1,9},{5,13},{25,17},{29,21},{2,10},{... | collective-permute-start | bytes 1572872 | tf_op jit(solution)/shard_map/ppermute | solution.py:440
  83.6 24.4 %collective-permute-start.6 = (bf16[512,512]{1,0:T(8,128)(2,1)S(1)}, bf16[512,512]{1,0:T(8,128)(2,1)S(1)}, u32[]{:S(2)}, u32[]{:S(2)}) collective-permute-start(bf16[512,512]{1,0:T(8,128)(2,1)S(1)} %convolution_convert_fusion.3), channel_id=1, source_target_pairs={{0,8},{4,12},{24,16},{28,20},{1,9},{5,13},{25,17},{29,21},{2,10},{... | collective-permute-start | bytes 1572872 | tf_op jit(solution)/shard_map/ppermute | solution.py:440
  87.6 31.7 %collective-permute-start.9 = (bf16[512,512]{1,0:T(8,128)(2,1)S(1)}, bf16[512,512]{1,0:T(8,128)(2,1)S(1)}, u32[]{:S(2)}, u32[]{:S(2)}) collective-permute-start(bf16[512,512]{1,0:T(8,128)(2,1)S(1)} %convolution_convert_fusion.2), channel_id=1, source_target_pairs={{0,8},{4,12},{24,16},{28,20},{1,9},{5,13},{25,17},{29,21},{2,10},{... | collective-permute-start | bytes 1572872 | tf_op jit(solution)/shard_map/ppermute | solution.py:440
  89.4 20.0 %collective-permute-start.16 = (bf16[512,512]{1,0:T(8,128)(2,1)S(1)}, bf16[512,512]{1,0:T(8,128)(2,1)S(1)}, u32[]{:S(2)}, u32[]{:S(2)}) collective-permute-start(bf16[512,512]{1,0:T(8,128)(2,1)S(1)} %fusion.12), channel_id=1, source_target_pairs={{8,16},{12,20},{16,8},{20,12},{9,17},{13,21},{17,9},{21,13},{10,18... | collective-permute-start | bytes 1572872 | tf_op jit(solution)/shard_map/ppermute | solution.py:440
  97.2 36.6 %collective-permute-start.19 = (bf16[512,512]{1,0:T(8,128)(2,1)S(1)}, bf16[512,512]{1,0:T(8,128)(2,1)}, u32[]{:S(2)}, u32[]{:S(2)}) collective-permute-start(bf16[512,512]{1,0:T(8,128)(2,1)S(1)} %fusion.13), channel_id=1, source_target_pairs={{8,16},{12,20},{16,8},{20,12},{9,17},{13,21},{17,9},{21,13},{10,18... | collective-permute-start | bytes 1572872 | tf_op jit(solution)/shard_map/ppermute | solution.py:440
  110.6 23.2 %collective-permute-start.17 = (bf16[512,512]{1,0:T(8,128)(2,1)}, bf16[512,512]{1,0:T(8,128)(2,1)}, u32[]{:S(2)}, u32[]{:S(2)}) collective-permute-start(bf16[512,512]{1,0:T(8,128)(2,1)} %fusion.11), channel_id=1, source_target_pairs={{0,8},{4,12},{8,0},{12,4},{16,24},{20,28},{24,16},{28,20},{1,9},{5... | collective-permute-start | bytes 1572872 | tf_op jit(solution)/shard_map/ppermute | solution.py:440
  123.2 18.6 %collective-permute-start.8 = (bf16[512,512]{1,0:T(8,128)(2,1)}, bf16[512,512]{1,0:T(8,128)(2,1)}, u32[]{:S(2)}, u32[]{:S(2)}) collective-permute-start(bf16[512,512]{1,0:T(8,128)(2,1)} %fusion.7), channel_id=1, source_target_pairs={{0,8},{4,12},{8,0},{12,4},{16,24},{20,28},{24,16},{28,20},{1,9},{5... | collective-permute-start | bytes 1572872 | tf_op jit(solution)/shard_map/ppermute | solution.py:440
  143.6 19.9 %collective-permute-start.11 = (bf16[512,512]{1,0:T(8,128)(2,1)S(1)}, bf16[512,512]{1,0:T(8,128)(2,1)S(1)}, u32[]{:S(2)}, u32[]{:S(2)}) collective-permute-start(bf16[512,512]{1,0:T(8,128)(2,1)S(1)} %fusion.6.refs_0_), channel_id=1, source_target_pairs={{0,8},{4,12},{8,0},{12,4},{16,24},{20,28},{24,16},{28,20},{1,9},{5... | collective-permute-start | bytes 1572872 | tf_op jit(solution)/shard_map/ppermute | solution.py:440
  146.1 18.0 %collective-permute-start.25 = (bf16[512,512]{1,0:T(8,128)(2,1)S(1)}, bf16[512,512]{1,0:T(8,128)(2,1)S(1)}, u32[]{:S(2)}, u32[]{:S(2)}) collective-permute-start(bf16[512,512]{1,0:T(8,128)(2,1)S(1)} %fusion.10.refs_0_), channel_id=1, source_target_pairs={{8,16},{12,20},{16,8},{20,12},{9,17},{13,21},{17,9},{21,13},{10,18... | collective-permute-start | bytes 1572872 | tf_op jit(solution)/shard_map/ppermute | solution.py:440
  146.8 18.6 %collective-permute-start.23 = (bf16[512,512]{1,0:T(8,128)(2,1)S(1)}, bf16[512,512]{1,0:T(8,128)(2,1)S(1)}, u32[]{:S(2)}, u32[]{:S(2)}) collective-permute-start(bf16[512,512]{1,0:T(8,128)(2,1)S(1)} %fusion.6.refs_0_), channel_id=1, source_target_pairs={{8,16},{12,20},{16,8},{20,12},{9,17},{13,21},{17,9},{21,13},{10,18... | collective-permute-start | bytes 1572872 | tf_op jit(solution)/shard_map/ppermute | solution.py:440
  164.1 19.3 %collective-permute-start.26 = (bf16[512,512]{1,0:T(8,128)(2,1)S(1)}, bf16[512,512]{1,0:T(8,128)(2,1)S(1)}, u32[]{:S(2)}, u32[]{:S(2)}) collective-permute-start(bf16[512,512]{1,0:T(8,128)(2,1)S(1)} %collective-permute-done.25.refs_2_), channel_id=1, source_target_pairs={{8,0},{12,4},{16,24},{20,28},{9,1},{13,5},{17,25},{21,29},{10,2},{... | collective-permute-start | bytes 1572872 | tf_op jit(solution)/shard_map/ppermute | solution.py:440
  165.5 29.2 %collective-permute-start.24 = (bf16[512,512]{1,0:T(8,128)(2,1)S(1)}, bf16[512,512]{1,0:T(8,128)(2,1)S(1)}, u32[]{:S(2)}, u32[]{:S(2)}) collective-permute-start(bf16[512,512]{1,0:T(8,128)(2,1)S(1)} %collective-permute-done.23.refs_2_), channel_id=1, source_target_pairs={{8,0},{12,4},{16,24},{20,28},{9,1},{13,5},{17,25},{21,29},{10,2},{... | collective-permute-start | bytes 1572872 | tf_op jit(solution)/shard_map/ppermute | solution.py:440
  166.8 39.2 %collective-permute-start.22 = (bf16[512,512]{1,0:T(8,128)(2,1)S(1)}, bf16[512,512]{1,0:T(8,128)(2,1)S(1)}, u32[]{:S(2)}, u32[]{:S(2)}) collective-permute-start(bf16[512,512]{1,0:T(8,128)(2,1)S(1)} %collective-permute-done.21.refs_2_), channel_id=1, source_target_pairs={{8,0},{12,4},{16,24},{20,28},{9,1},{13,5},{17,25},{21,29},{10,2},{... | collective-permute-start | bytes 1572872 | tf_op jit(solution)/shard_map/ppermute | solution.py:440
  168.1 47.5 %collective-permute-start.13 = (bf16[512,512]{1,0:T(8,128)(2,1)S(1)}, bf16[512,512]{1,0:T(8,128)(2,1)S(1)}, u32[]{:S(2)}, u32[]{:S(2)}) collective-permute-start(bf16[512,512]{1,0:T(8,128)(2,1)S(1)} %collective-permute-done.12.refs_2_), channel_id=1, source_target_pairs={{8,0},{12,4},{16,24},{20,28},{9,1},{13,5},{17,25},{21,29},{10,2},{... | collective-permute-start | bytes 1572872 | tf_op jit(solution)/shard_map/ppermute | solution.py:440
  220.2 23.3 %collective-permute-start.37 = (bf16[2,256,2,256]{3,2,1,0:T(2,128)(2,1)S(1)}, bf16[2,256,2,256]{3,2,1,0:T(2,128)(2,1)S(1)}, u32[]{:S(2)}, u32[]{:S(2)}) collective-permute-start(bf16[2,256,2,256]{3,2,1,0:T(2,128)(2,1)S(1)} %get-tuple-element.46), channel_id=1, source_target_pairs={{0,4},{4,0},{8,12},{12,8},{16,20},{20,16},{24,28},{28,24},{1,5},{5... | collective-permute-start | bytes 1572872 | tf_op jit(solution)/shard_map/ppermute | solution.py:22
  227.4 45.5 %collective-permute-start.33 = (bf16[2,256,2,256]{3,2,1,0:T(2,128)(2,1)S(1)}, bf16[2,256,2,256]{3,2,1,0:T(2,128)(2,1)S(1)}, u32[]{:S(2)}, u32[]{:S(2)}) collective-permute-start(bf16[2,256,2,256]{3,2,1,0:T(2,128)(2,1)S(1)} %get-tuple-element.42), channel_id=1, source_target_pairs={{0,4},{4,0},{8,12},{12,8},{16,20},{20,16},{24,28},{28,24},{1,5},{5... | collective-permute-start | bytes 1572872 | tf_op jit(solution)/shard_map/ppermute | solution.py:22
  227.4 31.4 %collective-permute-start.38 = (bf16[1,256,2,256]{3,2,1,0:T(2,128)(2,1)S(1)}, bf16[1,256,2,256]{3,2,1,0:T(2,128)(2,1)S(1)}, u32[]{:S(2)}, u32[]{:S(2)}) collective-permute-start(bf16[1,256,2,256]{3,2,1,0:T(2,128)(2,1)S(1)} %get-tuple-element.47), channel_id=1, source_target_pairs={{0,4},{4,0},{8,12},{12,8},{16,20},{20,16},{24,28},{28,24},{1,5},{5... | collective-permute-start | bytes 786440 | tf_op jit(solution)/shard_map/ppermute | solution.py:22
  236.4 28.1 %collective-permute-start.39 = (bf16[1,256,2,256]{3,2,1,0:T(2,128)(2,1)S(1)}, bf16[1,256,2,256]{3,2,1,0:T(2,128)(2,1)S(1)}, u32[]{:S(2)}, u32[]{:S(2)}) collective-permute-start(bf16[1,256,2,256]{3,2,1,0:T(2,128)(2,1)S(1)} %get-tuple-element.48), channel_id=1, source_target_pairs={{0,4},{4,0},{8,12},{12,8},{16,20},{20,16},{24,28},{28,24},{1,5},{5... | collective-permute-start | bytes 786440 | tf_op jit(solution)/shard_map/ppermute | solution.py:22
  243.5 29.4 %collective-permute-start.32 = (bf16[1,256,2,256]{3,2,1,0:T(2,128)(2,1)S(1)}, bf16[1,256,2,256]{3,2,1,0:T(2,128)(2,1)S(1)}, u32[]{:S(2)}, u32[]{:S(2)}) collective-permute-start(bf16[1,256,2,256]{3,2,1,0:T(2,128)(2,1)S(1)} %get-tuple-element.41), channel_id=1, source_target_pairs={{0,4},{4,0},{8,12},{12,8},{16,20},{20,16},{24,28},{28,24},{1,5},{5... | collective-permute-start | bytes 786440 | tf_op jit(solution)/shard_map/ppermute | solution.py:22
  258.9 21.4 %collective-permute-start.35 = (bf16[1,256,2,256]{3,2,1,0:T(2,128)(2,1)S(1)}, bf16[1,256,2,256]{3,2,1,0:T(2,128)(2,1)S(1)}, u32[]{:S(2)}, u32[]{:S(2)}) collective-permute-start(bf16[1,256,2,256]{3,2,1,0:T(2,128)(2,1)S(1)} %get-tuple-element.44), channel_id=1, source_target_pairs={{0,4},{4,0},{8,12},{12,8},{16,20},{20,16},{24,28},{28,24},{1,5},{5... | collective-permute-start | bytes 786440 | tf_op jit(solution)/shard_map/ppermute | solution.py:22
  (31 other events, 419.6 us)

commit v3 on v2

--- a/solution.py
+++ b/solution.py
@@ -12,7 +12,7 @@
 
 F32 = jnp.float32
 BF16 = jnp.bfloat16
-ENDS = 1
+ENDS = 3
 CHAINS = 2
 FLATS = 4
 
@@ -133,24 +133,26 @@
             copy.wait()
 
 
-def place(groups, table, at, held):
+def place(groups, table, at, shape, held):
     sizes = [g.shape[0] for g in groups]
     body = functools.partial(place_kernel, len(groups), at, sizes)
+    operands = list(groups)
+    specs = [pl.BlockSpec(memory_space=pltpu.VMEM)] * len(groups)
+    aliases = {}
+    if held is not None:
+        operands.append(held)
+        specs.append(pl.BlockSpec(memory_space=pl.ANY))
+        aliases = {len(operands): 0}
     return pl.pallas_call(
         body,
-        grid_spec=pltpu.PrefetchScalarGridSpec(
-            num_scalar_prefetch=1,
-            grid=(1,),
-            in_specs=[pl.BlockSpec(g.shape, lambda i, t: (0, 0, 0, 0)) for g in groups]
-            + [pl.BlockSpec(memory_space=pl.ANY)],
-            out_specs=pl.BlockSpec(memory_space=pl.ANY),
-            scratch_shapes=[pltpu.SemaphoreType.DMA((sum(sizes),))],
-        ),
-        out_shape=jax.ShapeDtypeStruct(held.shape, held.dtype),
-        input_output_aliases={len(groups) + 1: 0},
+        in_specs=[pl.BlockSpec(memory_space=pltpu.SMEM)] + specs,
+        out_specs=pl.BlockSpec(memory_space=pl.ANY),
+        scratch_shapes=[pltpu.SemaphoreType.DMA((sum(sizes),))],
+        out_shape=jax.ShapeDtypeStruct(shape, BF16),
+        input_output_aliases=aliases,
         compiler_params=limits(16),
         cost_estimate=cost(0, 4 * sum(g.size for g in groups)),
-    )(table, *groups, held)
+    )(table, *operands)
 
 
 def goal_kernel(ends, units, at, table, resid, bias, out):
@@ -169,6 +171,7 @@
 def goals_of(resid, bias, table, at, chains, ends, units, part):
     tokens, layers, _ = resid.shape
     wide = units // 2 * part
+    rows = tokens // 4
 
     def block(i, t):
         return t[at] + 2 * i
@@ -177,17 +180,17 @@
         functools.partial(goal_kernel, ends, units // 2, at),
         grid_spec=pltpu.PrefetchScalarGridSpec(
             num_scalar_prefetch=1,
-            grid=(chains,),
+            grid=(chains, 4),
             in_specs=[
-                pl.BlockSpec((tokens, layers, wide), lambda i, t: (0, 0, block(i, t))),
-                pl.BlockSpec((layers, wide), lambda i, t: (0, block(i, t))),
+                pl.BlockSpec((rows, layers, wide), lambda i, j, t: (j, 0, block(i, t))),
+                pl.BlockSpec((layers, wide), lambda i, j, t: (0, block(i, t))),
             ],
             out_specs=pl.BlockSpec(
-                (1, ends, tokens, layers * part), lambda i, t: (i, 0, 0, 0)
+                (1, ends, rows, layers * part), lambda i, j, t: (i, 0, j, 0)
             ),
         ),
         out_shape=jax.ShapeDtypeStruct((chains, ends, tokens, layers * part), F32),
-        compiler_params=limits(24),
+        compiler_params=limits(12),
         cost_estimate=cost(0, 6 * chains * ends * tokens * layers * part),
     )(table, resid, bias)
 
@@ -217,78 +220,67 @@
     )(resid)
 
 
-def use_kernel(n, scale, at, has_sum, table, act_t, weights, *refs):
-    errs, rest = refs[:n], refs[n:]
-    near, far, total = rest[-3:]
-    step = pl.program_id(0)
-    base = at + 4 * step
-    src, valid = table[base], table[base + 2]
-    if n == 1:
-        e = errs[0][...]
+def use_kernel(kinds, n, scale, at, has_sum, table, act_t, *refs):
+    m = len(kinds)
+    weights, errs, rest = refs[0], refs[1 : n + 1], refs[n + 1 :]
+    near, far, total, given = rest[-4:]
+    feats, layers, part = near.shape[1:]
+    cols = layers * part
+    found, added = [], []
+    for i, kind in enumerate(kinds):
+        entry = at + 3 * i
+        e = errs[kind[0]][...]
+        for j in kind[1:]:
+            e = jnp.where(table[entry] == j, errs[j][...], e)
+        found.append(e)
+        added.append(e * table[entry + 2].astype(BF16) if 0 in kind[1:] else e)
+
+    def grads(i, e):
+        grad = (dot(act_t[...], e, ((1,), (0,))) * scale).astype(BF16)
+        for layer in range(layers):
+            columns = slice(layer * part, (layer + 1) * part)
+            near[i, :, layer, :] = grad[:feats, columns]
+            far[i, :, layer, :] = grad[feats:, columns]
+
+    if m == 1:
+        grads(0, found[0])
     else:
-        e = jnp.where(src == 0, errs[0][...], errs[1][...])
-        for j in range(2, n):
-            e = jnp.where(src == j, errs[j][...], e)
-    feats, layers, part = near.shape
-    grad = (dot(act_t[...], e, ((1,), (0,))) * scale).astype(BF16)
-    for layer in range(layers):
-        columns = slice(layer * part, (layer + 1) * part)
-        near[:, layer, :] = grad[:feats, columns]
-        far[0, :, layer, :] = grad[feats:, columns]
-    more = dot(e, weights[0], ((1,), (1,))) * valid.astype(F32)
-
-    @pl.when(step == 0)
-    def _():
-        total[...] = rest[0][...] + more if has_sum else more
-
-    @pl.when(step > 0)
-    def _():
-        total[...] += more
-
-
-def use_of(act_t, weights, errs, total, held, table, at, m, shape, scale):
+        given[...] = jnp.concatenate(found, 1)
+
+        def one(i, _):
+            grads(i, given[:, pl.ds(pl.multiple_of(i * cols, cols), cols)])
+            return 0
+
+        lax.fori_loop(0, m, one, 0)
+    e = jnp.concatenate(added, 1)
+    w = jnp.concatenate([weights[table[at + 3 * i + 1]] for i in range(m)], 1)
+    more = dot(e, w, ((1,), (1,)))
+    total[...] = rest[0][...] + more if has_sum else more
+
+
+def use_of(act_t, weights, errs, total, table, at, kinds, shape, scale):
     feats, layers, _ = shape
     _, double, cols = weights.shape
     tokens = act_t.shape[1]
+    m, n = len(kinds), len(errs)
     part = cols // layers
-    whole = lambda a: pl.BlockSpec(a.shape, lambda i, t: (0, 0))
-    specs = [
-        whole(act_t),
-        pl.BlockSpec((1, double, cols), lambda i, t: (t[at + 4 * i + 1], 0, 0)),
-        *[whole(e) for e in errs],
+
+    outs = [
+        jax.ShapeDtypeStruct((m, feats, layers, part), BF16),
+        jax.ShapeDtypeStruct((m, feats, layers, part), BF16),
+        jax.ShapeDtypeStruct((tokens, double), F32),
     ]
     operands = [act_t, weights, *errs]
-    aliases = {}
     if total is not None:
-        specs.append(whole(total))
         operands.append(total)
-        aliases[len(operands)] = 2
-    if held is not None:
-        specs.append(pl.BlockSpec(memory_space=pl.ANY))
-        operands.append(held)
-        aliases[len(operands)] = 0
-    body = functools.partial(use_kernel, len(errs), scale, at, total is not None)
-    return pl.pallas_call(
-        body,
-        grid_spec=pltpu.PrefetchScalarGridSpec(
-            num_scalar_prefetch=1,
-            grid=(m,),
-            in_specs=specs,
-            out_specs=[
-                pl.BlockSpec(
-                    (feats, layers, part), lambda i, t: (0, 0, t[at + 4 * i + 3])
-                ),
-                pl.BlockSpec((1, feats, layers, part), lambda i, t: (i, 0, 0, 0)),
-                pl.BlockSpec((tokens, double), lambda i, t: (0, 0)),
-            ],
-        ),
-        out_shape=[
-            jax.ShapeDtypeStruct(shape, BF16),
-            jax.ShapeDtypeStruct((m, feats, layers, part), BF16),
-            jax.ShapeDtypeStruct((tokens, double), F32),
-        ],
-        input_output_aliases=aliases,
-        compiler_params=limits(24),
+    near_by = pl.BlockSpec(memory_space=pltpu.VMEM)
+    return pl.pallas_call(
+        functools.partial(use_kernel, kinds, n, scale, at, total is not None),
+        in_specs=[pl.BlockSpec(memory_space=pltpu.SMEM)] + [near_by] * len(operands),
+        out_specs=[near_by] * 3,
+        out_shape=outs,
+        scratch_shapes=[pltpu.VMEM((tokens, m * cols), BF16)],
+        compiler_params=limits(28),
         cost_estimate=cost(
             4 * m * tokens * double * cols, 2 * m * cols * (tokens + 2 * double)
         ),
@@ -353,27 +345,26 @@
         add("goals_at", [(centre + sign * e) % (units // 2) for e in range(ends)])
         add("edges", [int(pos in (0, line - 1))] * chains * ends)
         for k in range(chains):
-            base = (side * chains + k) * units
             for i, group in enumerate(groups):
                 values = []
-                came = [e for e in group if e[0]]
+                came = sorted({s for s, _ in group if s})
                 for s, d in group:
                     way, unit, valid = taken(s, d)
                     src = 0
                     if way:
-                        src = 1 + 2 * sorted({e[0] for e in came}).index(s)
+                        src = 1 + 2 * came.index(s)
                         src += int((way < 0) == (pos % 2 == 0))
-                    values += [src, unit, valid, base + unit]
+                    values += [src, unit, valid]
                 add(f"use_{k}_{i}", values)
-        for k in range(chains):
-            base = ((1 - side) * chains + k) * units
             values = []
-            for s, d in sum(groups, []):
-                _, unit, valid = taken(s, d)
-                if d and not 0 <= centre + d * s < units:
-                    valid = 0
-                values += [base + unit, valid]
-            add(f"far_{k}", values)
+            for group in groups:
+                for of in (side, 1 - side):
+                    for s, d in group:
+                        _, unit, valid = taken(s, d)
+                        if d and not 0 <= centre + d * s < units:
+                            valid = 0
+                        values += [(of * chains + k) * units + unit, valid]
+            add(f"place_{k}", values)
         rows.append(row)
     return np.array(rows, np.int32), at
 
@@ -479,14 +470,11 @@
                 errs[k][late] = err.astype(BF16)
 
     dact = dec_grad = None
-    fars = [[] for _ in range(chains)]
+    grads = [[] for _ in range(chains)]
     groups = groups_of(units, steps)
     ahead = [errs[k][0] for k in range(chains)]
     behind = [errs[k][0] for k in range(chains)]
     came = [[] for _ in range(chains)]
-
-    def put(name, which, dec_grad):
-        return place(which, table, at[name], dec_grad)
 
     for s in range(steps + 1):
         ways = range(max(s - ends, 0), line - 1), range(1, line + min(ends - s, 0))
@@ -502,37 +490,45 @@
             for i, group in enumerate(groups):
                 if group[-1][0] != s:
                     continue
-                dec_grad, far, dact = use_of(
+                first = sorted({t for t, _ in group if t})
+                kinds = [
+                    (0,)
+                    if not t
+                    else tuple(1 + 2 * first.index(t) + j for j in range(2))
+                    + (() if d else (0,))
+                    for t, d in group
+                ]
+                near, far, dact = use_of(
                     act_t,
                     both[k],
                     [errs[k][0], *came[k]],
                     dact,
-                    dec_grad,
                     table,
                     at[f"use_{k}_{i}"],
-                    len(group),
+                    kinds,
                     dec_weight.shape,
                     scale,
                 )
                 came[k] = []
-                fars[k].append(swap(far, "layer", 0))
+                grads[k] += [near, swap(far, "layer", 0)]
     for k in range(chains):
-        dec_grad = put(f"far_{k}", fars[k], dec_grad)
+        dec_grad = place(grads[k], table, at[f"place_{k}"], dec_weight.shape, dec_grad)
 
     flats = []
     for i in range(FLATS):
         flats.append(flat_of(resid, i, FLATS, 4))
 
-    for b in range(bits):
-        stay, go = halves(dact, ups[b])
-        come = swap(go.astype(BF16), "cuts", b).astype(F32)
-        dact = stay + come
+    stay, go = halves(dact, ups[0])
+    come = swap(go.astype(BF16), "cuts", 0).astype(F32)
+    dact = stay + come
     come = swap(dact[:, feats:].astype(BF16), "layer", 0).astype(F32)
     dact = dact[:, :feats] + come
-    dz = jnp.where(act_mine > 0, dact * scale, 0.0).astype(BF16)
-    for b in reversed(range(bits)):
-        come = swap(dz, "cuts", b)
-        dz = joined(dz, come, ups[b])
+    for b in range(1, bits):
+        dact = dact + swap(dact.astype(BF16), "cuts", b).astype(F32)
+    live, _ = halves(act[:, :feats], ups[0])
+    dz = jnp.where(live > 0, dact * scale, 0.0).astype(BF16)
+    come = swap(dz, "cuts", 0)
+    dz = joined(dz, come, ups[0])
     enc_grad = enc_grad_of(flats, dz, 2)
     return enc_grad, dec_grad
 

time: 288 us -> 276 us (0.958)
  waiting for transfers between devices: 150 us -> 101 us
  starting transfers between devices: 50.6 us -> 81.2 us
  Pallas kernels: 46.9 us -> 52.1 us
    ppermute x20 -> x36, waiting for transfers between devices: 68.1 us -> 37.7 us  [exchange(): return lax.ppermute(value, 'layer', pairs)]
    ppermute x20 -> x36, starting transfers between devices: 34.8 us -> 63.9 us  [exchange(): return lax.ppermute(value, 'layer', pairs)]
    ppermute x20 -> x19, waiting for transfers between devices: 82.3 us -> 63.4 us  [swap(): return lax.ppermute(value, axis, [(i, i ^ 1 << bit) for i in range(size)])]
    ppermute x20 -> x19, starting transfers between devices: 15.8 us -> 17.3 us  [swap(): return lax.ppermute(value, axis, [(i, i ^ 1 << bit) for i in range(size)])]
    unnamed x30 -> x24, local copies, waits for them, and re-layouts: 12.9 us -> 11.9 us
    dot_general x13 -> x25, matrix products: 19.7 us -> 19 us  [dot(): return lax.dot_general(a, b, (dims, ((), ())), preferred_element_type=F32)]
  transfers between devices with their start and end apart: 40 -> 55, of which waited for: 22 -> 21; matrix products, arithmetic and copies ran while one was open for 5% -> 6% of each run, Pallas kernels for 14% -> 17%
where the time goes in v3:
time: 276 us; the launch traced here: 274 us
  waiting for transfers between devices  101 us (37%)
  starting transfers between devices  81.2 us (29%)
  Pallas kernels  52.1 us (19%)
  matrix products  19 us (7%)
  local copies, waits for them, and re-layouts  12.6 us (5%)
  other arithmetic  6.4 us (2%)
    ppermute x36, starting transfers between devices, exchange(): return lax.ppermute(value, 'layer', pairs)  63.9 us
    ppermute x19, waiting for transfers between devices, swap(): return lax.ppermute(value, axis, [(i, i ^ 1 << bit) for i in range(size)])  63.4 us
    ppermute x36, waiting for transfers between devices, exchange(): return lax.ppermute(value, 'layer', pairs)  37.7 us
    pallas_call x8, Pallas kernels, use_of(): pl.pallas_call(functools.partial(use_kernel, kinds, n, scale, at, total i...  22.6 us
    dot_general x25, matrix products, dot(): return lax.dot_general(a, b, (dims, ((), ())), preferred_element_type=F32)  19 us
    ppermute x19, starting transfers between devices, swap(): return lax.ppermute(value, axis, [(i, i ^ 1 << bit) for i in range(size)])  17.3 us
    unnamed x24, local copies, waits for them, and re-layouts  11.9 us
    pallas_call x4, Pallas kernels, prep(): pl.pallas_call(prep_kernel, grid_spec=pltpu.PrefetchScalarGridSpec(num_sc...  8.69 us
  transfers between devices with their start and end apart: 55, of which 21 were waited for; matrix products, arithmetic and copies ran while one was open for 6% of the time, Pallas kernels for 17%

profile of v3, /device:TPU:0, one launch (start us, length us, event | category | flops | bytes accessed | tf_op | source)
XLA Modules:
  0.0 273.9 jit_solution(94127741279428460)
XLA Ops:
  0.6 9.3 %fusion.2 = f32[512,256]{1,0:T(8,128)S(1)} fusion(bf16[2,4096,256]{2,1,0:T(8,128)(2,1)} %param.7, bf16[512,2,4096]{2,1,0:T(2,128)(2,1)} %resid.1), kind=kOutput, calls=%fused_computation.4 | convolution fusion | flops 2147483648 | bytes 13107200 | tf_op jit(solution)/shard_map/dot_general | solution.py:40
  16.0 3.8 %shard_map.86 = bf16[1,8,256,256]{3,2,1,0:T(8,128)(2,1)} custom-call(s32[140]{0:T(256)} %bitcast.138, bf16[256,2,4096]{2,1,0:T(2,128)(2,1)} %rows.15), custom_call_target="tpu_custom_call" | custom-call | bytes 2097152 | tf_op jit(solution)/shard_map/pallas_call | solution.py:95
  21.9 24.4 %collective-permute-done.2 = bf16[128,256]{1,0:T(8,128)(2,1)S(1)} collective-permute-done((bf16[128,256]{1,0:T(8,128)(2,1)S(1)}, bf16[128,256]{1,0:T(8,128)(2,1)S(1)}, u32[]{:S(2)}, u32[]{:S(2)}) %collective-permute-start.2) | collective-permute-done | bytes 65568 | tf_op jit(solution)/shard_map/ppermute | solution.py:22
  65.4 5.0 %shard_map.84 = f32[2,3,512,256]{3,2,1,0:T(8,128)S(1)} custom-call(s32[140]{0:T(256)S(1)} %bitcast.142, bf16[512,2,4096]{2,1,0:T(2,128)(2,1)S(1)} %copy-done, f32[2,4096]{1,0:T(2,128)S(1)} %copy-done.8), custom_call_target="tpu_custom_call" | custom-call | bytes 4718592 | tf_op jit(solution)/shard_map/pallas_call | solution.py:179
  85.5 4.6 %collective-permute-done.26 = bf16[512,256]{1,0:T(8,128)(2,1)S(1)} collective-permute-done((bf16[512,256]{1,0:T(8,128)(2,1)S(1)}, bf16[512,256]{1,0:T(8,128)(2,1)S(1)}, u32[]{:S(2)}, u32[]{:S(2)}) %collective-permute-start.26) | collective-permute-done | bytes 262176 | tf_op jit(solution)/shard_map/ppermute | solution.py:431
  91.1 4.6 %collective-permute-done.6 = bf16[512,256]{1,0:T(8,128)(2,1)S(1)} collective-permute-done((bf16[512,256]{1,0:T(8,128)(2,1)S(1)}, bf16[512,256]{1,0:T(8,128)(2,1)S(1)}, u32[]{:S(2)}, u32[]{:S(2)}) %collective-permute-start.6) | collective-permute-done | bytes 262176 | tf_op jit(solution)/shard_map/ppermute | solution.py:431
  96.9 3.9 %collective-permute-done.11 = bf16[512,256]{1,0:T(8,128)(2,1)S(1)} collective-permute-done((bf16[512,256]{1,0:T(8,128)(2,1)S(1)}, bf16[512,256]{1,0:T(8,128)(2,1)S(1)}, u32[]{:S(2)}, u32[]{:S(2)}) %collective-permute-start.11) | collective-permute-done | bytes 262176 | tf_op jit(solution)/shard_map/ppermute | solution.py:431
  102.2 5.3 %collective-permute-start.23 = (bf16[512,256]{1,0:T(8,128)(2,1)S(1)}, bf16[512,256]{1,0:T(8,128)(2,1)S(1)}, u32[]{:S(2)}, u32[]{:S(2)}) collective-permute-start(bf16[512,256]{1,0:T(8,128)(2,1)S(1)} %fusion.29), channel_id=1, source_target_pairs={{0,8},{4,12},{8,0},{12,4},{16,24},{20,28},{24,16},{28,20},{1,9},{5... | collective-permute-start | bytes 786440 | tf_op jit(solution)/shard_map/ppermute | solution.py:431
  115.7 4.6 %collective-permute-done.28 = bf16[512,256]{1,0:T(8,128)(2,1)S(1)} collective-permute-done((bf16[512,256]{1,0:T(8,128)(2,1)S(1)}, bf16[512,256]{1,0:T(8,128)(2,1)S(1)}, u32[]{:S(2)}, u32[]{:S(2)}) %collective-permute-start.28) | collective-permute-done | bytes 262176 | tf_op jit(solution)/shard_map/ppermute | solution.py:431
  121.3 4.6 %collective-permute-done.8 = bf16[512,256]{1,0:T(8,128)(2,1)S(1)} collective-permute-done((bf16[512,256]{1,0:T(8,128)(2,1)S(1)}, bf16[512,256]{1,0:T(8,128)(2,1)S(1)}, u32[]{:S(2)}, u32[]{:S(2)}) %collective-permute-start.8) | collective-permute-done | bytes 262176 | tf_op jit(solution)/shard_map/ppermute | solution.py:431
  139.2 3.9 %collective-permute-done.25 = bf16[512,256]{1,0:T(8,128)(2,1)S(1)} collective-permute-done((bf16[512,256]{1,0:T(8,128)(2,1)S(1)}, bf16[512,256]{1,0:T(8,128)(2,1)S(1)}, u32[]{:S(2)}, u32[]{:S(2)}) %collective-permute-start.25) | collective-permute-done | bytes 262176 | tf_op jit(solution)/shard_map/ppermute | solution.py:431
  144.0 4.9 %collective-permute-start.30 = (bf16[512,256]{1,0:T(8,128)(2,1)S(1)}, bf16[512,256]{1,0:T(8,128)(2,1)S(1)}, u32[]{:S(2)}, u32[]{:S(2)}) collective-permute-start(bf16[512,256]{1,0:T(8,128)(2,1)S(1)} %fusion.26.refs_1_), channel_id=1, source_target_pairs={{0,8},{4,12},{8,0},{12,4},{16,24},{20,28},{24,16},{28,20},{1,9},{5... | collective-permute-start | bytes 786440 | tf_op jit(solution)/shard_map/ppermute | solution.py:431
  149.9 4.6 %collective-permute-start.15 = (bf16[512,256]{1,0:T(8,128)(2,1)S(1)}, bf16[512,256]{1,0:T(8,128)(2,1)S(1)}, u32[]{:S(2)}, u32[]{:S(2)}) collective-permute-start(bf16[512,256]{1,0:T(8,128)(2,1)S(1)} %fusion.17.refs_1_), channel_id=1, source_target_pairs={{0,8},{4,12},{8,0},{12,4},{16,24},{20,28},{24,16},{28,20},{1,9},{5... | collective-permute-start | bytes 786440 | tf_op jit(solution)/shard_map/ppermute | solution.py:431
  157.0 3.9 %collective-permute-start.40 = (bf16[512,256]{1,0:T(8,128)(2,1)S(1)}, bf16[512,256]{1,0:T(8,128)(2,1)S(1)}, u32[]{:S(2)}, u32[]{:S(2)}) collective-permute-start(bf16[512,256]{1,0:T(8,128)(2,1)S(1)} %add.255.refs_3_), channel_id=1, source_target_pairs={{0,8},{4,12},{8,0},{12,4},{16,24},{20,28},{24,16},{28,20},{1,9},{5... | collective-permute-start | bytes 786440 | tf_op jit(solution)/shard_map/ppermute | solution.py:431
  162.4 4.6 %collective-permute-start.32 = (bf16[512,256]{1,0:T(8,128)(2,1)S(1)}, bf16[512,256]{1,0:T(8,128)(2,1)S(1)}, u32[]{:S(2)}, u32[]{:S(2)}) collective-permute-start(bf16[512,256]{1,0:T(8,128)(2,1)S(1)} %add.246.refs_5_), channel_id=1, source_target_pairs={{0,8},{4,12},{8,0},{12,4},{16,24},{20,28},{24,16},{28,20},{1,9},{5... | collective-permute-start | bytes 786440 | tf_op jit(solution)/shard_map/ppermute | solution.py:431
  168.0 5.4 %collective-permute-start.17 = (bf16[512,256]{1,0:T(8,128)(2,1)S(1)}, bf16[512,256]{1,0:T(8,128)(2,1)S(1)}, u32[]{:S(2)}, u32[]{:S(2)}) collective-permute-start(bf16[512,256]{1,0:T(8,128)(2,1)S(1)} %add.232.refs_5_), channel_id=1, source_target_pairs={{0,8},{4,12},{8,0},{12,4},{16,24},{20,28},{24,16},{28,20},{1,9},{5... | collective-permute-start | bytes 786440 | tf_op jit(solution)/shard_map/ppermute | solution.py:431
  174.8 3.6 %collective-permute-done.32.refs_2_ = bf16[512,256]{1,0:T(8,128)(2,1)S(1)} collective-permute-done((bf16[512,256]{1,0:T(8,128)(2,1)S(1)}, bf16[512,256]{1,0:T(8,128)(2,1)S(1)}, u32[]{:S(2)}, u32[]{:S(2)}) %collective-permute-start.32) | collective-permute-done | bytes 262176 | tf_op jit(solution)/shard_map/ppermute | solution.py:431
  189.0 4.6 %shard_map.89 = (bf16[4,256,2,128]{3,2,1,0:T(2,128)(2,1)S(1)}, bf16[4,256,2,128]{3,2,1,0:T(2,128)(2,1)S(1)}, f32[512,512]{1,0:T(8,128)S(1)}) custom-call(s32[140]{0:T(256)S(1)} %bitcast.145, bf16[512,512]{1,0:T(8,128)(2,1)S(1)} %shard_map.81.act_t, bf16[8,512,256]{2,1,0:T(8,128)(2,1)S(1)} %pad_maximum_fusion.1.refs_0_, bf16[512,256]{1,0:T(8,128)(2,1)S(1)} %fusion.26.refs_1_, ...), custom_call_target="tpu_custom_call" | custom-call | flops 1073741824 | bytes 3145728 | tf_op jit(solution)/shard_map/pallas_call | solution.py:277
  195.2 4.6 %shard_map.90 = (bf16[4,256,2,128]{3,2,1,0:T(2,128)(2,1)S(1)}, bf16[4,256,2,128]{3,2,1,0:T(2,128)(2,1)S(1)}, f32[512,512]{1,0:T(8,128)S(1)}) custom-call(s32[140]{0:T(256)S(1)} %bitcast.146, bf16[512,512]{1,0:T(8,128)(2,1)S(1)} %shard_map.81.act_t, bf16[8,512,256]{2,1,0:T(8,128)(2,1)S(1)} %pad_maximum_fusion.refs_0_, bf16[512,256]{1,0:T(8,128)(2,1)S(1)} %fusion.17.refs_1_, ...), custom_call_target="tpu_custom_call" | custom-call | flops 1073741824 | bytes 3145728 | tf_op jit(solution)/shard_map/pallas_call | solution.py:277
  199.8 3.6 %shard_map.91 = (bf16[3,256,2,128]{3,2,1,0:T(2,128)(2,1)S(1)}, bf16[3,256,2,128]{3,2,1,0:T(2,128)(2,1)S(1)}, f32[512,512]{1,0:T(8,128)S(1)}) custom-call(s32[140]{0:T(256)S(1)} %bitcast.147, bf16[512,512]{1,0:T(8,128)(2,1)S(1)} %shard_map.81.act_t, bf16[8,512,256]{2,1,0:T(8,128)(2,1)S(1)} %pad_maximum_fusion.1.refs_0_, bf16[512,256]{1,0:T(8,128)(2,1)S(1)} %fusion.26.refs_1_, ...), custom_call_target="tpu_custom_call" | custom-call | flops 805306368 | bytes 2359296 | tf_op jit(solution)/shard_map/pallas_call | solution.py:277
  203.5 3.6 %shard_map.92 = (bf16[3,256,2,128]{3,2,1,0:T(2,128)(2,1)S(1)}, bf16[3,256,2,128]{3,2,1,0:T(2,128)(2,1)S(1)}, f32[512,512]{1,0:T(8,128)S(1)}) custom-call(s32[140]{0:T(256)S(1)} %bitcast.148, bf16[512,512]{1,0:T(8,128)(2,1)S(1)} %shard_map.81.act_t, bf16[8,512,256]{2,1,0:T(8,128)(2,1)S(1)} %pad_maximum_fusion.refs_0_, bf16[512,256]{1,0:T(8,128)(2,1)S(1)} %fusion.17.refs_1_, ...), custom_call_target="tpu_custom_call" | custom-call | flops 805306368 | bytes 2359296 | tf_op jit(solution)/shard_map/pallas_call | solution.py:277
  216.2 11.9 %collective-permute-done.44 = bf16[256,256]{1,0:T(8,128)(2,1)S(1)} collective-permute-done((bf16[256,256]{1,0:T(8,128)(2,1)S(1)}, bf16[256,256]{1,0:T(8,128)(2,1)S(1)}, u32[]{:S(2)}, u32[]{:S(2)}) %collective-permute-start.44) | collective-permute-done | bytes 131104 | tf_op jit(solution)/shard_map/ppermute | solution.py:22
  232.9 20.4 %collective-permute-done.54.refs_7_ = bf16[1,256,2,128]{3,2,1,0:T(2,128)(2,1)S(1)} collective-permute-done((bf16[1,256,2,128]{3,2,1,0:T(2,128)(2,1)S(1)}, bf16[1,256,2,128]{3,2,1,0:T(2,128)(2,1)S(1)}, u32[]{:S(2)}, u32[]{:S(2)}) %collective-permute-start.54) | collective-permute-done | bytes 131104 | tf_op jit(solution)/shard_map/ppermute | solution.py:22
  269.0 4.9 %shard_map.95 = bf16[2,4096,256]{2,1,0:T(8,128)(2,1)} custom-call(bf16[2,128,4096]{2,1,0:T(8,128)(2,1)S(1)} %shard_map.77.refs_0_, bf16[2,128,4096]{2,1,0:T(8,128)(2,1)S(1)} %shard_map.78.refs_1_, bf16[2,128,4096]{2,1,0:T(8,128)(2,1)S(1)} %shard_map.79.refs_2_, bf16[2,128,4096]{2,1,0:T(8,128)(2,1)S(1)} %shard_map.80.refs_3_, ...), custom_call_target="tpu_custom_call" | custom-call | flops 2147483648 | bytes 12582912 | tf_op jit(solution)/shard_map/pallas_call | solution.py:61
  (178 shorter events, 117.4 us)
Async XLA Ops:
  19.7 52.6 %collective-permute-start.20 = (bf16[8,256,256]{2,1,0:T(8,128)(2,1)}, bf16[8,256,256]{2,1,0:T(8,128)(2,1)}, u32[]{:S(2)}, u32[]{:S(2)}) collective-permute-start(bf16[8,256,256]{2,1,0:T(8,128)(2,1)} %bitcast.153), channel_id=1, source_target_pairs={{0,4},{4,0},{8,12},{12,8},{16,20},{20,16},{24,28},{28,24},{1,5},{5... | collective-permute-start | bytes 3145736 | tf_op jit(solution)/shard_map/ppermute | solution.py:22
  21.3 25.0 %collective-permute-start.2 = (bf16[128,256]{1,0:T(8,128)(2,1)S(1)}, bf16[128,256]{1,0:T(8,128)(2,1)S(1)}, u32[]{:S(2)}, u32[]{:S(2)}) collective-permute-start(bf16[128,256]{1,0:T(8,128)(2,1)S(1)} %maximum_convert_fusion), channel_id=1, source_target_pairs={{0,4},{4,0},{8,12},{12,8},{16,20},{20,16},{24,28},{28,24},{1,5},{5... | collective-permute-start | bytes 196616 | tf_op jit(solution)/shard_map/ppermute | solution.py:22
  51.2 28.3 %collective-permute-start.5 = (bf16[8,256,256]{2,1,0:T(8,128)(2,1)}, bf16[8,256,256]{2,1,0:T(8,128)(2,1)}, u32[]{:S(2)}, u32[]{:S(2)}) collective-permute-start(bf16[8,256,256]{2,1,0:T(8,128)(2,1)} %bitcast.5), channel_id=1, source_target_pairs={{0,4},{4,0},{8,12},{12,8},{16,20},{20,16},{24,28},{28,24},{1,5},{5... | collective-permute-start | bytes 3145736 | tf_op jit(solution)/shard_map/ppermute | solution.py:22
  53.0 18.2 %collective-permute-start.4 = (bf16[256,512]{1,0:T(8,128)(2,1)S(1)}, bf16[256,512]{1,0:T(8,128)(2,1)}, u32[]{:S(2)}, u32[]{:S(2)}) collective-permute-start(bf16[256,512]{1,0:T(8,128)(2,1)S(1)} %maximum_select_fusion.1), channel_id=1, source_target_pairs={{0,1},{1,0},{2,3},{3,2},{4,5},{5,4},{6,7},{7,6},{8,9},{9,8},{10,11... | collective-permute-start | bytes 786440 | tf_op jit(solution)/shard_map/ppermute | solution.py:22
  82.8 18.1 %collective-permute-start.11 = (bf16[512,256]{1,0:T(8,128)(2,1)S(1)}, bf16[512,256]{1,0:T(8,128)(2,1)S(1)}, u32[]{:S(2)}, u32[]{:S(2)}) collective-permute-start(bf16[512,256]{1,0:T(8,128)(2,1)S(1)} %convolution_convert_fusion.2), channel_id=1, source_target_pairs={{0,8},{4,12},{24,16},{28,20},{1,9},{5,13},{25,17},{29,21},{2,10},{... | collective-permute-start | bytes 786440 | tf_op jit(solution)/shard_map/ppermute | solution.py:431
  84.8 17.0 %collective-permute-start.22 = (bf16[512,256]{1,0:T(8,128)(2,1)S(1)}, bf16[512,256]{1,0:T(8,128)(2,1)S(1)}, u32[]{:S(2)}, u32[]{:S(2)}) collective-permute-start(bf16[512,256]{1,0:T(8,128)(2,1)S(1)} %fusion.30), channel_id=1, source_target_pairs={{8,16},{12,20},{16,8},{20,12},{9,17},{13,21},{17,9},{21,13},{10,18... | collective-permute-start | bytes 786440 | tf_op jit(solution)/shard_map/ppermute | solution.py:431
  90.4 17.1 %collective-permute-start.27 = (bf16[512,256]{1,0:T(8,128)(2,1)S(1)}, bf16[512,256]{1,0:T(8,128)(2,1)S(1)}, u32[]{:S(2)}, u32[]{:S(2)}) collective-permute-start(bf16[512,256]{1,0:T(8,128)(2,1)S(1)} %fusion.33), channel_id=1, source_target_pairs={{8,16},{12,20},{16,8},{20,12},{9,17},{13,21},{17,9},{21,13},{10,18... | collective-permute-start | bytes 786440 | tf_op jit(solution)/shard_map/ppermute | solution.py:431
  108.2 17.7 %collective-permute-start.8 = (bf16[512,256]{1,0:T(8,128)(2,1)S(1)}, bf16[512,256]{1,0:T(8,128)(2,1)S(1)}, u32[]{:S(2)}, u32[]{:S(2)}) collective-permute-start(bf16[512,256]{1,0:T(8,128)(2,1)S(1)} %fusion.20), channel_id=1, source_target_pairs={{0,8},{4,12},{8,0},{12,4},{16,24},{20,28},{24,16},{28,20},{1,9},{5... | collective-permute-start | bytes 786440 | tf_op jit(solution)/shard_map/ppermute | solution.py:431
  110.6 19.6 %collective-permute-start.13 = (bf16[512,256]{1,0:T(8,128)(2,1)S(1)}, bf16[512,256]{1,0:T(8,128)(2,1)S(1)}, u32[]{:S(2)}, u32[]{:S(2)}) collective-permute-start(bf16[512,256]{1,0:T(8,128)(2,1)S(1)} %fusion.23), channel_id=1, source_target_pairs={{0,8},{4,12},{8,0},{12,4},{16,24},{20,28},{24,16},{28,20},{1,9},{5... | collective-permute-start | bytes 786440 | tf_op jit(solution)/shard_map/ppermute | solution.py:431
  115.0 17.0 %collective-permute-start.24 = (bf16[512,256]{1,0:T(8,128)(2,1)S(1)}, bf16[512,256]{1,0:T(8,128)(2,1)S(1)}, u32[]{:S(2)}, u32[]{:S(2)}) collective-permute-start(bf16[512,256]{1,0:T(8,128)(2,1)S(1)} %fusion.28), channel_id=1, source_target_pairs={{8,16},{12,20},{16,8},{20,12},{9,17},{13,21},{17,9},{21,13},{10,18... | collective-permute-start | bytes 786440 | tf_op jit(solution)/shard_map/ppermute | solution.py:431
  120.6 18.6 %collective-permute-start.29 = (bf16[512,256]{1,0:T(8,128)(2,1)S(1)}, bf16[512,256]{1,0:T(8,128)(2,1)S(1)}, u32[]{:S(2)}, u32[]{:S(2)}) collective-permute-start(bf16[512,256]{1,0:T(8,128)(2,1)S(1)} %fusion.31), channel_id=1, source_target_pairs={{8,16},{12,20},{16,8},{20,12},{9,17},{13,21},{17,9},{21,13},{10,18... | collective-permute-start | bytes 786440 | tf_op jit(solution)/shard_map/ppermute | solution.py:431
  130.5 18.4 %collective-permute-start.14 = (bf16[512,256]{1,0:T(8,128)(2,1)S(1)}, bf16[512,256]{1,0:T(8,128)(2,1)S(1)}, u32[]{:S(2)}, u32[]{:S(2)}) collective-permute-start(bf16[512,256]{1,0:T(8,128)(2,1)S(1)} %fusion.22), channel_id=1, source_target_pairs={{8,16},{12,20},{16,8},{20,12},{9,17},{13,21},{17,9},{21,13},{10,18... | collective-permute-start | bytes 786440 | tf_op jit(solution)/shard_map/ppermute | solution.py:431
  157.0 16.5 %collective-permute-start.40 = (bf16[512,256]{1,0:T(8,128)(2,1)S(1)}, bf16[512,256]{1,0:T(8,128)(2,1)S(1)}, u32[]{:S(2)}, u32[]{:S(2)}) collective-permute-start(bf16[512,256]{1,0:T(8,128)(2,1)S(1)} %add.255.refs_3_), channel_id=1, source_target_pairs={{0,8},{4,12},{8,0},{12,4},{16,24},{20,28},{24,16},{28,20},{1,9},{5... | collective-permute-start | bytes 786440 | tf_op jit(solution)/shard_map/ppermute | solution.py:431
  162.4 16.0 %collective-permute-start.32 = (bf16[512,256]{1,0:T(8,128)(2,1)S(1)}, bf16[512,256]{1,0:T(8,128)(2,1)S(1)}, u32[]{:S(2)}, u32[]{:S(2)}) collective-permute-start(bf16[512,256]{1,0:T(8,128)(2,1)S(1)} %add.246.refs_5_), channel_id=1, source_target_pairs={{0,8},{4,12},{8,0},{12,4},{16,24},{20,28},{24,16},{28,20},{1,9},{5... | collective-permute-start | bytes 786440 | tf_op jit(solution)/shard_map/ppermute | solution.py:431
  181.9 17.9 %collective-permute-start.42 = (bf16[512,256]{1,0:T(8,128)(2,1)S(1)}, bf16[512,256]{1,0:T(8,128)(2,1)S(1)}, u32[]{:S(2)}, u32[]{:S(2)}) collective-permute-start(bf16[512,256]{1,0:T(8,128)(2,1)S(1)} %collective-permute-done.41.refs_3_), channel_id=1, source_target_pairs={{8,0},{12,4},{16,24},{20,28},{9,1},{13,5},{17,25},{21,29},{10,2},{... | collective-permute-start | bytes 786440 | tf_op jit(solution)/shard_map/ppermute | solution.py:431
  186.4 17.1 %collective-permute-start.38 = (bf16[512,256]{1,0:T(8,128)(2,1)S(1)}, bf16[512,256]{1,0:T(8,128)(2,1)S(1)}, u32[]{:S(2)}, u32[]{:S(2)}) collective-permute-start(bf16[512,256]{1,0:T(8,128)(2,1)S(1)} %collective-permute-done.37.refs_3_), channel_id=1, source_target_pairs={{8,0},{12,4},{16,24},{20,28},{9,1},{13,5},{17,25},{21,29},{10,2},{... | collective-permute-start | bytes 786440 | tf_op jit(solution)/shard_map/ppermute | solution.py:431
  187.7 19.4 %collective-permute-start.34 = (bf16[512,256]{1,0:T(8,128)(2,1)S(1)}, bf16[512,256]{1,0:T(8,128)(2,1)S(1)}, u32[]{:S(2)}, u32[]{:S(2)}) collective-permute-start(bf16[512,256]{1,0:T(8,128)(2,1)S(1)} %collective-permute-done.33.refs_5_), channel_id=1, source_target_pairs={{8,0},{12,4},{16,24},{20,28},{9,1},{13,5},{17,25},{21,29},{10,2},{... | collective-permute-start | bytes 786440 | tf_op jit(solution)/shard_map/ppermute | solution.py:431
  210.4 22.0 %collective-permute-start.52 = (bf16[4,256,2,128]{3,2,1,0:T(2,128)(2,1)S(1)}, bf16[4,256,2,128]{3,2,1,0:T(2,128)(2,1)S(1)}, u32[]{:S(2)}, u32[]{:S(2)}) collective-permute-start(bf16[4,256,2,128]{3,2,1,0:T(2,128)(2,1)S(1)} %get-tuple-element.45), channel_id=1, source_target_pairs={{0,4},{4,0},{8,12},{12,8},{16,20},{20,16},{24,28},{28,24},{1,5},{5... | collective-permute-start | bytes 1572872 | tf_op jit(solution)/shard_map/ppermute | solution.py:22
  212.7 18.2 %collective-permute-start.51 = (bf16[1,256,2,128]{3,2,1,0:T(2,128)(2,1)S(1)}, bf16[1,256,2,128]{3,2,1,0:T(2,128)(2,1)S(1)}, u32[]{:S(2)}, u32[]{:S(2)}) collective-permute-start(bf16[1,256,2,128]{3,2,1,0:T(2,128)(2,1)S(1)} %get-tuple-element.43), channel_id=1, source_target_pairs={{0,4},{4,0},{8,12},{12,8},{16,20},{20,16},{24,28},{28,24},{1,5},{5... | collective-permute-start | bytes 393224 | tf_op jit(solution)/shard_map/ppermute | solution.py:22
  214.2 50.4 %collective-permute-start.48 = (bf16[4,256,2,128]{3,2,1,0:T(2,128)(2,1)S(1)}, bf16[4,256,2,128]{3,2,1,0:T(2,128)(2,1)S(1)}, u32[]{:S(2)}, u32[]{:S(2)}) collective-permute-start(bf16[4,256,2,128]{3,2,1,0:T(2,128)(2,1)S(1)} %get-tuple-element.37), channel_id=1, source_target_pairs={{0,4},{4,0},{8,12},{12,8},{16,20},{20,16},{24,28},{28,24},{1,5},{5... | collective-permute-start | bytes 1572872 | tf_op jit(solution)/shard_map/ppermute | solution.py:22
  214.7 40.7 %collective-permute-start.53 = (bf16[3,256,2,128]{3,2,1,0:T(2,128)(2,1)S(1)}, bf16[3,256,2,128]{3,2,1,0:T(2,128)(2,1)S(1)}, u32[]{:S(2)}, u32[]{:S(2)}) collective-permute-start(bf16[3,256,2,128]{3,2,1,0:T(2,128)(2,1)S(1)} %get-tuple-element.47), channel_id=1, source_target_pairs={{0,4},{4,0},{8,12},{12,8},{16,20},{20,16},{24,28},{28,24},{1,5},{5... | collective-permute-start | bytes 1179656 | tf_op jit(solution)/shard_map/ppermute | solution.py:22
  228.1 25.3 %collective-permute-start.54 = (bf16[1,256,2,128]{3,2,1,0:T(2,128)(2,1)S(1)}, bf16[1,256,2,128]{3,2,1,0:T(2,128)(2,1)S(1)}, u32[]{:S(2)}, u32[]{:S(2)}) collective-permute-start(bf16[1,256,2,128]{3,2,1,0:T(2,128)(2,1)S(1)} %get-tuple-element.49), channel_id=1, source_target_pairs={{0,4},{4,0},{8,12},{12,8},{16,20},{20,16},{24,28},{28,24},{1,5},{5... | collective-permute-start | bytes 393224 | tf_op jit(solution)/shard_map/ppermute | solution.py:22
  230.9 23.0 %collective-permute-start.45 = (bf16[256,256]{1,0:T(8,128)(2,1)S(1)}, bf16[256,256]{1,0:T(8,128)(2,1)S(1)}, u32[]{:S(2)}, u32[]{:S(2)}) collective-permute-start(bf16[256,256]{1,0:T(8,128)(2,1)S(1)} %fusion.89), channel_id=1, source_target_pairs={{0,2},{1,3},{2,0},{3,1},{4,6},{5,7},{6,4},{7,5},{8,10},{9,11},{10,... | collective-permute-start | bytes 393224 | tf_op jit(solution)/shard_map/ppermute | solution.py:22
  232.4 34.4 %collective-permute-start.49 = (bf16[3,256,2,128]{3,2,1,0:T(2,128)(2,1)S(1)}, bf16[3,256,2,128]{3,2,1,0:T(2,128)(2,1)S(1)}, u32[]{:S(2)}, u32[]{:S(2)}) collective-permute-start(bf16[3,256,2,128]{3,2,1,0:T(2,128)(2,1)S(1)} %get-tuple-element.39), channel_id=1, source_target_pairs={{0,4},{4,0},{8,12},{12,8},{16,20},{20,16},{24,28},{28,24},{1,5},{5... | collective-permute-start | bytes 1179656 | tf_op jit(solution)/shard_map/ppermute | solution.py:22
  (43 other events, 490.0 us)

commit v4 on v3

--- a/solution.py
+++ b/solution.py
@@ -171,7 +171,6 @@
 def goals_of(resid, bias, table, at, chains, ends, units, part):
     tokens, layers, _ = resid.shape
     wide = units // 2 * part
-    rows = tokens // 4
 
     def block(i, t):
         return t[at] + 2 * i
@@ -180,17 +179,17 @@
         functools.partial(goal_kernel, ends, units // 2, at),
         grid_spec=pltpu.PrefetchScalarGridSpec(
             num_scalar_prefetch=1,
-            grid=(chains, 4),
+            grid=(chains,),
             in_specs=[
-                pl.BlockSpec((rows, layers, wide), lambda i, j, t: (j, 0, block(i, t))),
-                pl.BlockSpec((layers, wide), lambda i, j, t: (0, block(i, t))),
+                pl.BlockSpec((tokens, layers, wide), lambda i, t: (0, 0, block(i, t))),
+                pl.BlockSpec((layers, wide), lambda i, t: (0, block(i, t))),
             ],
             out_specs=pl.BlockSpec(
-                (1, ends, rows, layers * part), lambda i, j, t: (i, 0, j, 0)
+                (1, ends, tokens, layers * part), lambda i, t: (i, 0, 0, 0)
             ),
         ),
         out_shape=jax.ShapeDtypeStruct((chains, ends, tokens, layers * part), F32),
-        compiler_params=limits(12),
+        compiler_params=limits(24),
         cost_estimate=cost(0, 6 * chains * ends * tokens * layers * part),
     )(table, resid, bias)
 

time: 276 us -> 276 us (level)
  no operation moved by 1% of the time
where the time goes in v4:
time: 276 us; the launch traced here: 274 us
  waiting for transfers between devices  101 us (37%)
  starting transfers between devices  81 us (29%)
  Pallas kernels  51.8 us (19%)
  matrix products  19 us (7%)
  local copies, waits for them, and re-layouts  12.6 us (5%)
  other arithmetic  6.4 us (2%)
    ppermute x36, starting transfers between devices, exchange(): return lax.ppermute(value, 'layer', pairs)  63.8 us
    ppermute x19, waiting for transfers between devices, swap(): return lax.ppermute(value, axis, [(i, i ^ 1 << bit) for i in range(size)])  63.5 us
    ppermute x36, waiting for transfers between devices, exchange(): return lax.ppermute(value, 'layer', pairs)  37.8 us
    pallas_call x8, Pallas kernels, use_of(): pl.pallas_call(functools.partial(use_kernel, kinds, n, scale, at, total i...  22.6 us
    dot_general x25, matrix products, dot(): return lax.dot_general(a, b, (dims, ((), ())), preferred_element_type=F32)  19 us
    ppermute x19, starting transfers between devices, swap(): return lax.ppermute(value, axis, [(i, i ^ 1 << bit) for i in range(size)])  17.2 us
    unnamed x24, local copies, waits for them, and re-layouts  11.9 us
    pallas_call x4, Pallas kernels, prep(): pl.pallas_call(prep_kernel, grid_spec=pltpu.PrefetchScalarGridSpec(num_sc...  8.69 us
  transfers between devices with their start and end apart: 55, of which 21 were waited for; matrix products, arithmetic and copies ran while one was open for 6% of the time, Pallas kernels for 17%

profile of v4, /device:TPU:0, one launch (start us, length us, event | category | flops | bytes accessed | tf_op | source)
XLA Modules:
  0.0 273.5 jit_solution(14286109201278779348)
XLA Ops:
  0.6 9.3 %fusion.2 = f32[512,256]{1,0:T(8,128)S(1)} fusion(bf16[2,4096,256]{2,1,0:T(8,128)(2,1)} %param.7, bf16[512,2,4096]{2,1,0:T(2,128)(2,1)} %resid.1), kind=kOutput, calls=%fused_computation.4 | convolution fusion | flops 2147483648 | bytes 13107200 | tf_op jit(solution)/shard_map/dot_general | solution.py:40
  16.0 3.8 %shard_map.86 = bf16[1,8,256,256]{3,2,1,0:T(8,128)(2,1)} custom-call(s32[140]{0:T(256)} %bitcast.138, bf16[256,2,4096]{2,1,0:T(2,128)(2,1)} %rows.15), custom_call_target="tpu_custom_call" | custom-call | bytes 2097152 | tf_op jit(solution)/shard_map/pallas_call | solution.py:95
  21.9 24.4 %collective-permute-done.2 = bf16[128,256]{1,0:T(8,128)(2,1)S(1)} collective-permute-done((bf16[128,256]{1,0:T(8,128)(2,1)S(1)}, bf16[128,256]{1,0:T(8,128)(2,1)S(1)}, u32[]{:S(2)}, u32[]{:S(2)}) %collective-permute-start.2) | collective-permute-done | bytes 65568 | tf_op jit(solution)/shard_map/ppermute | solution.py:22
  65.4 4.6 %shard_map.84 = f32[2,3,512,256]{3,2,1,0:T(8,128)S(1)} custom-call(s32[140]{0:T(256)S(1)} %bitcast.142, bf16[512,2,4096]{2,1,0:T(2,128)(2,1)S(1)} %copy-done, f32[2,4096]{1,0:T(2,128)S(1)} %copy-done.8), custom_call_target="tpu_custom_call" | custom-call | bytes 4718592 | tf_op jit(solution)/shard_map/pallas_call | solution.py:178
  85.1 4.6 %collective-permute-done.26 = bf16[512,256]{1,0:T(8,128)(2,1)S(1)} collective-permute-done((bf16[512,256]{1,0:T(8,128)(2,1)S(1)}, bf16[512,256]{1,0:T(8,128)(2,1)S(1)}, u32[]{:S(2)}, u32[]{:S(2)}) %collective-permute-start.26) | collective-permute-done | bytes 262176 | tf_op jit(solution)/shard_map/ppermute | solution.py:430
  90.8 4.6 %collective-permute-done.6 = bf16[512,256]{1,0:T(8,128)(2,1)S(1)} collective-permute-done((bf16[512,256]{1,0:T(8,128)(2,1)S(1)}, bf16[512,256]{1,0:T(8,128)(2,1)S(1)}, u32[]{:S(2)}, u32[]{:S(2)}) %collective-permute-start.6) | collective-permute-done | bytes 262176 | tf_op jit(solution)/shard_map/ppermute | solution.py:430
  96.4 4.1 %collective-permute-done.11 = bf16[512,256]{1,0:T(8,128)(2,1)S(1)} collective-permute-done((bf16[512,256]{1,0:T(8,128)(2,1)S(1)}, bf16[512,256]{1,0:T(8,128)(2,1)S(1)}, u32[]{:S(2)}, u32[]{:S(2)}) %collective-permute-start.11) | collective-permute-done | bytes 262176 | tf_op jit(solution)/shard_map/ppermute | solution.py:430
  101.8 5.4 %collective-permute-start.23 = (bf16[512,256]{1,0:T(8,128)(2,1)S(1)}, bf16[512,256]{1,0:T(8,128)(2,1)S(1)}, u32[]{:S(2)}, u32[]{:S(2)}) collective-permute-start(bf16[512,256]{1,0:T(8,128)(2,1)S(1)} %fusion.29), channel_id=1, source_target_pairs={{0,8},{4,12},{8,0},{12,4},{16,24},{20,28},{24,16},{28,20},{1,9},{5... | collective-permute-start | bytes 786440 | tf_op jit(solution)/shard_map/ppermute | solution.py:430
  115.3 4.6 %collective-permute-done.28 = bf16[512,256]{1,0:T(8,128)(2,1)S(1)} collective-permute-done((bf16[512,256]{1,0:T(8,128)(2,1)S(1)}, bf16[512,256]{1,0:T(8,128)(2,1)S(1)}, u32[]{:S(2)}, u32[]{:S(2)}) %collective-permute-start.28) | collective-permute-done | bytes 262176 | tf_op jit(solution)/shard_map/ppermute | solution.py:430
  120.9 4.6 %collective-permute-done.8 = bf16[512,256]{1,0:T(8,128)(2,1)S(1)} collective-permute-done((bf16[512,256]{1,0:T(8,128)(2,1)S(1)}, bf16[512,256]{1,0:T(8,128)(2,1)S(1)}, u32[]{:S(2)}, u32[]{:S(2)}) %collective-permute-start.8) | collective-permute-done | bytes 262176 | tf_op jit(solution)/shard_map/ppermute | solution.py:430
  138.8 3.9 %collective-permute-done.25 = bf16[512,256]{1,0:T(8,128)(2,1)S(1)} collective-permute-done((bf16[512,256]{1,0:T(8,128)(2,1)S(1)}, bf16[512,256]{1,0:T(8,128)(2,1)S(1)}, u32[]{:S(2)}, u32[]{:S(2)}) %collective-permute-start.25) | collective-permute-done | bytes 262176 | tf_op jit(solution)/shard_map/ppermute | solution.py:430
  143.7 4.9 %collective-permute-start.30 = (bf16[512,256]{1,0:T(8,128)(2,1)S(1)}, bf16[512,256]{1,0:T(8,128)(2,1)S(1)}, u32[]{:S(2)}, u32[]{:S(2)}) collective-permute-start(bf16[512,256]{1,0:T(8,128)(2,1)S(1)} %fusion.26.refs_1_), channel_id=1, source_target_pairs={{0,8},{4,12},{8,0},{12,4},{16,24},{20,28},{24,16},{28,20},{1,9},{5... | collective-permute-start | bytes 786440 | tf_op jit(solution)/shard_map/ppermute | solution.py:430
  149.5 4.6 %collective-permute-start.15 = (bf16[512,256]{1,0:T(8,128)(2,1)S(1)}, bf16[512,256]{1,0:T(8,128)(2,1)S(1)}, u32[]{:S(2)}, u32[]{:S(2)}) collective-permute-start(bf16[512,256]{1,0:T(8,128)(2,1)S(1)} %fusion.17.refs_1_), channel_id=1, source_target_pairs={{0,8},{4,12},{8,0},{12,4},{16,24},{20,28},{24,16},{28,20},{1,9},{5... | collective-permute-start | bytes 786440 | tf_op jit(solution)/shard_map/ppermute | solution.py:430
  156.6 3.9 %collective-permute-start.40 = (bf16[512,256]{1,0:T(8,128)(2,1)S(1)}, bf16[512,256]{1,0:T(8,128)(2,1)S(1)}, u32[]{:S(2)}, u32[]{:S(2)}) collective-permute-start(bf16[512,256]{1,0:T(8,128)(2,1)S(1)} %add.255.refs_3_), channel_id=1, source_target_pairs={{0,8},{4,12},{8,0},{12,4},{16,24},{20,28},{24,16},{28,20},{1,9},{5... | collective-permute-start | bytes 786440 | tf_op jit(solution)/shard_map/ppermute | solution.py:430
  162.1 4.6 %collective-permute-start.32 = (bf16[512,256]{1,0:T(8,128)(2,1)S(1)}, bf16[512,256]{1,0:T(8,128)(2,1)S(1)}, u32[]{:S(2)}, u32[]{:S(2)}) collective-permute-start(bf16[512,256]{1,0:T(8,128)(2,1)S(1)} %add.246.refs_5_), channel_id=1, source_target_pairs={{0,8},{4,12},{8,0},{12,4},{16,24},{20,28},{24,16},{28,20},{1,9},{5... | collective-permute-start | bytes 786440 | tf_op jit(solution)/shard_map/ppermute | solution.py:430
  167.7 5.4 %collective-permute-start.17 = (bf16[512,256]{1,0:T(8,128)(2,1)S(1)}, bf16[512,256]{1,0:T(8,128)(2,1)S(1)}, u32[]{:S(2)}, u32[]{:S(2)}) collective-permute-start(bf16[512,256]{1,0:T(8,128)(2,1)S(1)} %add.232.refs_5_), channel_id=1, source_target_pairs={{0,8},{4,12},{8,0},{12,4},{16,24},{20,28},{24,16},{28,20},{1,9},{5... | collective-permute-start | bytes 786440 | tf_op jit(solution)/shard_map/ppermute | solution.py:430
  174.4 3.7 %collective-permute-done.32.refs_2_ = bf16[512,256]{1,0:T(8,128)(2,1)S(1)} collective-permute-done((bf16[512,256]{1,0:T(8,128)(2,1)S(1)}, bf16[512,256]{1,0:T(8,128)(2,1)S(1)}, u32[]{:S(2)}, u32[]{:S(2)}) %collective-permute-start.32) | collective-permute-done | bytes 262176 | tf_op jit(solution)/shard_map/ppermute | solution.py:430
  188.7 4.6 %shard_map.89 = (bf16[4,256,2,128]{3,2,1,0:T(2,128)(2,1)S(1)}, bf16[4,256,2,128]{3,2,1,0:T(2,128)(2,1)S(1)}, f32[512,512]{1,0:T(8,128)S(1)}) custom-call(s32[140]{0:T(256)S(1)} %bitcast.145, bf16[512,512]{1,0:T(8,128)(2,1)S(1)} %shard_map.81.act_t, bf16[8,512,256]{2,1,0:T(8,128)(2,1)S(1)} %pad_maximum_fusion.1.refs_0_, bf16[512,256]{1,0:T(8,128)(2,1)S(1)} %fusion.26.refs_1_, ...), custom_call_target="tpu_custom_call" | custom-call | flops 1073741824 | bytes 3145728 | tf_op jit(solution)/shard_map/pallas_call | solution.py:276
  194.8 4.6 %shard_map.90 = (bf16[4,256,2,128]{3,2,1,0:T(2,128)(2,1)S(1)}, bf16[4,256,2,128]{3,2,1,0:T(2,128)(2,1)S(1)}, f32[512,512]{1,0:T(8,128)S(1)}) custom-call(s32[140]{0:T(256)S(1)} %bitcast.146, bf16[512,512]{1,0:T(8,128)(2,1)S(1)} %shard_map.81.act_t, bf16[8,512,256]{2,1,0:T(8,128)(2,1)S(1)} %pad_maximum_fusion.refs_0_, bf16[512,256]{1,0:T(8,128)(2,1)S(1)} %fusion.17.refs_1_, ...), custom_call_target="tpu_custom_call" | custom-call | flops 1073741824 | bytes 3145728 | tf_op jit(solution)/shard_map/pallas_call | solution.py:276
  199.5 3.6 %shard_map.91 = (bf16[3,256,2,128]{3,2,1,0:T(2,128)(2,1)S(1)}, bf16[3,256,2,128]{3,2,1,0:T(2,128)(2,1)S(1)}, f32[512,512]{1,0:T(8,128)S(1)}) custom-call(s32[140]{0:T(256)S(1)} %bitcast.147, bf16[512,512]{1,0:T(8,128)(2,1)S(1)} %shard_map.81.act_t, bf16[8,512,256]{2,1,0:T(8,128)(2,1)S(1)} %pad_maximum_fusion.1.refs_0_, bf16[512,256]{1,0:T(8,128)(2,1)S(1)} %fusion.26.refs_1_, ...), custom_call_target="tpu_custom_call" | custom-call | flops 805306368 | bytes 2359296 | tf_op jit(solution)/shard_map/pallas_call | solution.py:276
  203.2 3.6 %shard_map.92 = (bf16[3,256,2,128]{3,2,1,0:T(2,128)(2,1)S(1)}, bf16[3,256,2,128]{3,2,1,0:T(2,128)(2,1)S(1)}, f32[512,512]{1,0:T(8,128)S(1)}) custom-call(s32[140]{0:T(256)S(1)} %bitcast.148, bf16[512,512]{1,0:T(8,128)(2,1)S(1)} %shard_map.81.act_t, bf16[8,512,256]{2,1,0:T(8,128)(2,1)S(1)} %pad_maximum_fusion.refs_0_, bf16[512,256]{1,0:T(8,128)(2,1)S(1)} %fusion.17.refs_1_, ...), custom_call_target="tpu_custom_call" | custom-call | flops 805306368 | bytes 2359296 | tf_op jit(solution)/shard_map/pallas_call | solution.py:276
  215.9 11.9 %collective-permute-done.44 = bf16[256,256]{1,0:T(8,128)(2,1)S(1)} collective-permute-done((bf16[256,256]{1,0:T(8,128)(2,1)S(1)}, bf16[256,256]{1,0:T(8,128)(2,1)S(1)}, u32[]{:S(2)}, u32[]{:S(2)}) %collective-permute-start.44) | collective-permute-done | bytes 131104 | tf_op jit(solution)/shard_map/ppermute | solution.py:22
  232.6 20.5 %collective-permute-done.54.refs_7_ = bf16[1,256,2,128]{3,2,1,0:T(2,128)(2,1)S(1)} collective-permute-done((bf16[1,256,2,128]{3,2,1,0:T(2,128)(2,1)S(1)}, bf16[1,256,2,128]{3,2,1,0:T(2,128)(2,1)S(1)}, u32[]{:S(2)}, u32[]{:S(2)}) %collective-permute-start.54) | collective-permute-done | bytes 131104 | tf_op jit(solution)/shard_map/ppermute | solution.py:22
  268.7 4.9 %shard_map.95 = bf16[2,4096,256]{2,1,0:T(8,128)(2,1)} custom-call(bf16[2,128,4096]{2,1,0:T(8,128)(2,1)S(1)} %shard_map.77.refs_0_, bf16[2,128,4096]{2,1,0:T(8,128)(2,1)S(1)} %shard_map.78.refs_1_, bf16[2,128,4096]{2,1,0:T(8,128)(2,1)S(1)} %shard_map.79.refs_2_, bf16[2,128,4096]{2,1,0:T(8,128)(2,1)S(1)} %shard_map.80.refs_3_, ...), custom_call_target="tpu_custom_call" | custom-call | flops 2147483648 | bytes 12582912 | tf_op jit(solution)/shard_map/pallas_call | solution.py:61
  (178 shorter events, 117.2 us)
Async XLA Ops:
  19.7 52.2 %collective-permute-start.20 = (bf16[8,256,256]{2,1,0:T(8,128)(2,1)}, bf16[8,256,256]{2,1,0:T(8,128)(2,1)}, u32[]{:S(2)}, u32[]{:S(2)}) collective-permute-start(bf16[8,256,256]{2,1,0:T(8,128)(2,1)} %bitcast.153), channel_id=1, source_target_pairs={{0,4},{4,0},{8,12},{12,8},{16,20},{20,16},{24,28},{28,24},{1,5},{5... | collective-permute-start | bytes 3145736 | tf_op jit(solution)/shard_map/ppermute | solution.py:22
  21.3 25.0 %collective-permute-start.2 = (bf16[128,256]{1,0:T(8,128)(2,1)S(1)}, bf16[128,256]{1,0:T(8,128)(2,1)S(1)}, u32[]{:S(2)}, u32[]{:S(2)}) collective-permute-start(bf16[128,256]{1,0:T(8,128)(2,1)S(1)} %maximum_convert_fusion), channel_id=1, source_target_pairs={{0,4},{4,0},{8,12},{12,8},{16,20},{20,16},{24,28},{28,24},{1,5},{5... | collective-permute-start | bytes 196616 | tf_op jit(solution)/shard_map/ppermute | solution.py:22
  51.2 28.1 %collective-permute-start.5 = (bf16[8,256,256]{2,1,0:T(8,128)(2,1)}, bf16[8,256,256]{2,1,0:T(8,128)(2,1)}, u32[]{:S(2)}, u32[]{:S(2)}) collective-permute-start(bf16[8,256,256]{2,1,0:T(8,128)(2,1)} %bitcast.5), channel_id=1, source_target_pairs={{0,4},{4,0},{8,12},{12,8},{16,20},{20,16},{24,28},{28,24},{1,5},{5... | collective-permute-start | bytes 3145736 | tf_op jit(solution)/shard_map/ppermute | solution.py:22
  53.0 17.8 %collective-permute-start.4 = (bf16[256,512]{1,0:T(8,128)(2,1)S(1)}, bf16[256,512]{1,0:T(8,128)(2,1)}, u32[]{:S(2)}, u32[]{:S(2)}) collective-permute-start(bf16[256,512]{1,0:T(8,128)(2,1)S(1)} %maximum_select_fusion.1), channel_id=1, source_target_pairs={{0,1},{1,0},{2,3},{3,2},{4,5},{5,4},{6,7},{7,6},{8,9},{9,8},{10,11... | collective-permute-start | bytes 786440 | tf_op jit(solution)/shard_map/ppermute | solution.py:22
  82.6 17.9 %collective-permute-start.11 = (bf16[512,256]{1,0:T(8,128)(2,1)S(1)}, bf16[512,256]{1,0:T(8,128)(2,1)S(1)}, u32[]{:S(2)}, u32[]{:S(2)}) collective-permute-start(bf16[512,256]{1,0:T(8,128)(2,1)S(1)} %convolution_convert_fusion.2), channel_id=1, source_target_pairs={{0,8},{4,12},{24,16},{28,20},{1,9},{5,13},{25,17},{29,21},{2,10},{... | collective-permute-start | bytes 786440 | tf_op jit(solution)/shard_map/ppermute | solution.py:430
  84.5 17.0 %collective-permute-start.22 = (bf16[512,256]{1,0:T(8,128)(2,1)S(1)}, bf16[512,256]{1,0:T(8,128)(2,1)S(1)}, u32[]{:S(2)}, u32[]{:S(2)}) collective-permute-start(bf16[512,256]{1,0:T(8,128)(2,1)S(1)} %fusion.30), channel_id=1, source_target_pairs={{8,16},{12,20},{16,8},{20,12},{9,17},{13,21},{17,9},{21,13},{10,18... | collective-permute-start | bytes 786440 | tf_op jit(solution)/shard_map/ppermute | solution.py:430
  90.1 17.1 %collective-permute-start.27 = (bf16[512,256]{1,0:T(8,128)(2,1)S(1)}, bf16[512,256]{1,0:T(8,128)(2,1)S(1)}, u32[]{:S(2)}, u32[]{:S(2)}) collective-permute-start(bf16[512,256]{1,0:T(8,128)(2,1)S(1)} %fusion.33), channel_id=1, source_target_pairs={{8,16},{12,20},{16,8},{20,12},{9,17},{13,21},{17,9},{21,13},{10,18... | collective-permute-start | bytes 786440 | tf_op jit(solution)/shard_map/ppermute | solution.py:430
  107.9 17.7 %collective-permute-start.8 = (bf16[512,256]{1,0:T(8,128)(2,1)S(1)}, bf16[512,256]{1,0:T(8,128)(2,1)S(1)}, u32[]{:S(2)}, u32[]{:S(2)}) collective-permute-start(bf16[512,256]{1,0:T(8,128)(2,1)S(1)} %fusion.20), channel_id=1, source_target_pairs={{0,8},{4,12},{8,0},{12,4},{16,24},{20,28},{24,16},{28,20},{1,9},{5... | collective-permute-start | bytes 786440 | tf_op jit(solution)/shard_map/ppermute | solution.py:430
  110.2 19.6 %collective-permute-start.13 = (bf16[512,256]{1,0:T(8,128)(2,1)S(1)}, bf16[512,256]{1,0:T(8,128)(2,1)S(1)}, u32[]{:S(2)}, u32[]{:S(2)}) collective-permute-start(bf16[512,256]{1,0:T(8,128)(2,1)S(1)} %fusion.23), channel_id=1, source_target_pairs={{0,8},{4,12},{8,0},{12,4},{16,24},{20,28},{24,16},{28,20},{1,9},{5... | collective-permute-start | bytes 786440 | tf_op jit(solution)/shard_map/ppermute | solution.py:430
  114.6 17.0 %collective-permute-start.24 = (bf16[512,256]{1,0:T(8,128)(2,1)S(1)}, bf16[512,256]{1,0:T(8,128)(2,1)S(1)}, u32[]{:S(2)}, u32[]{:S(2)}) collective-permute-start(bf16[512,256]{1,0:T(8,128)(2,1)S(1)} %fusion.28), channel_id=1, source_target_pairs={{8,16},{12,20},{16,8},{20,12},{9,17},{13,21},{17,9},{21,13},{10,18... | collective-permute-start | bytes 786440 | tf_op jit(solution)/shard_map/ppermute | solution.py:430
  120.2 18.5 %collective-permute-start.29 = (bf16[512,256]{1,0:T(8,128)(2,1)S(1)}, bf16[512,256]{1,0:T(8,128)(2,1)S(1)}, u32[]{:S(2)}, u32[]{:S(2)}) collective-permute-start(bf16[512,256]{1,0:T(8,128)(2,1)S(1)} %fusion.31), channel_id=1, source_target_pairs={{8,16},{12,20},{16,8},{20,12},{9,17},{13,21},{17,9},{21,13},{10,18... | collective-permute-start | bytes 786440 | tf_op jit(solution)/shard_map/ppermute | solution.py:430
  130.1 18.4 %collective-permute-start.14 = (bf16[512,256]{1,0:T(8,128)(2,1)S(1)}, bf16[512,256]{1,0:T(8,128)(2,1)S(1)}, u32[]{:S(2)}, u32[]{:S(2)}) collective-permute-start(bf16[512,256]{1,0:T(8,128)(2,1)S(1)} %fusion.22), channel_id=1, source_target_pairs={{8,16},{12,20},{16,8},{20,12},{9,17},{13,21},{17,9},{21,13},{10,18... | collective-permute-start | bytes 786440 | tf_op jit(solution)/shard_map/ppermute | solution.py:430
  156.6 16.4 %collective-permute-start.40 = (bf16[512,256]{1,0:T(8,128)(2,1)S(1)}, bf16[512,256]{1,0:T(8,128)(2,1)S(1)}, u32[]{:S(2)}, u32[]{:S(2)}) collective-permute-start(bf16[512,256]{1,0:T(8,128)(2,1)S(1)} %add.255.refs_3_), channel_id=1, source_target_pairs={{0,8},{4,12},{8,0},{12,4},{16,24},{20,28},{24,16},{28,20},{1,9},{5... | collective-permute-start | bytes 786440 | tf_op jit(solution)/shard_map/ppermute | solution.py:430
  162.1 16.0 %collective-permute-start.32 = (bf16[512,256]{1,0:T(8,128)(2,1)S(1)}, bf16[512,256]{1,0:T(8,128)(2,1)S(1)}, u32[]{:S(2)}, u32[]{:S(2)}) collective-permute-start(bf16[512,256]{1,0:T(8,128)(2,1)S(1)} %add.246.refs_5_), channel_id=1, source_target_pairs={{0,8},{4,12},{8,0},{12,4},{16,24},{20,28},{24,16},{28,20},{1,9},{5... | collective-permute-start | bytes 786440 | tf_op jit(solution)/shard_map/ppermute | solution.py:430
  181.6 17.9 %collective-permute-start.42 = (bf16[512,256]{1,0:T(8,128)(2,1)S(1)}, bf16[512,256]{1,0:T(8,128)(2,1)S(1)}, u32[]{:S(2)}, u32[]{:S(2)}) collective-permute-start(bf16[512,256]{1,0:T(8,128)(2,1)S(1)} %collective-permute-done.41.refs_3_), channel_id=1, source_target_pairs={{8,0},{12,4},{16,24},{20,28},{9,1},{13,5},{17,25},{21,29},{10,2},{... | collective-permute-start | bytes 786440 | tf_op jit(solution)/shard_map/ppermute | solution.py:430
  186.1 17.1 %collective-permute-start.38 = (bf16[512,256]{1,0:T(8,128)(2,1)S(1)}, bf16[512,256]{1,0:T(8,128)(2,1)S(1)}, u32[]{:S(2)}, u32[]{:S(2)}) collective-permute-start(bf16[512,256]{1,0:T(8,128)(2,1)S(1)} %collective-permute-done.37.refs_3_), channel_id=1, source_target_pairs={{8,0},{12,4},{16,24},{20,28},{9,1},{13,5},{17,25},{21,29},{10,2},{... | collective-permute-start | bytes 786440 | tf_op jit(solution)/shard_map/ppermute | solution.py:430
  187.4 19.4 %collective-permute-start.34 = (bf16[512,256]{1,0:T(8,128)(2,1)S(1)}, bf16[512,256]{1,0:T(8,128)(2,1)S(1)}, u32[]{:S(2)}, u32[]{:S(2)}) collective-permute-start(bf16[512,256]{1,0:T(8,128)(2,1)S(1)} %collective-permute-done.33.refs_5_), channel_id=1, source_target_pairs={{8,0},{12,4},{16,24},{20,28},{9,1},{13,5},{17,25},{21,29},{10,2},{... | collective-permute-start | bytes 786440 | tf_op jit(solution)/shard_map/ppermute | solution.py:430
  210.1 22.0 %collective-permute-start.52 = (bf16[4,256,2,128]{3,2,1,0:T(2,128)(2,1)S(1)}, bf16[4,256,2,128]{3,2,1,0:T(2,128)(2,1)S(1)}, u32[]{:S(2)}, u32[]{:S(2)}) collective-permute-start(bf16[4,256,2,128]{3,2,1,0:T(2,128)(2,1)S(1)} %get-tuple-element.45), channel_id=1, source_target_pairs={{0,4},{4,0},{8,12},{12,8},{16,20},{20,16},{24,28},{28,24},{1,5},{5... | collective-permute-start | bytes 1572872 | tf_op jit(solution)/shard_map/ppermute | solution.py:22
  212.4 18.2 %collective-permute-start.51 = (bf16[1,256,2,128]{3,2,1,0:T(2,128)(2,1)S(1)}, bf16[1,256,2,128]{3,2,1,0:T(2,128)(2,1)S(1)}, u32[]{:S(2)}, u32[]{:S(2)}) collective-permute-start(bf16[1,256,2,128]{3,2,1,0:T(2,128)(2,1)S(1)} %get-tuple-element.43), channel_id=1, source_target_pairs={{0,4},{4,0},{8,12},{12,8},{16,20},{20,16},{24,28},{28,24},{1,5},{5... | collective-permute-start | bytes 393224 | tf_op jit(solution)/shard_map/ppermute | solution.py:22
  213.8 50.4 %collective-permute-start.48 = (bf16[4,256,2,128]{3,2,1,0:T(2,128)(2,1)S(1)}, bf16[4,256,2,128]{3,2,1,0:T(2,128)(2,1)S(1)}, u32[]{:S(2)}, u32[]{:S(2)}) collective-permute-start(bf16[4,256,2,128]{3,2,1,0:T(2,128)(2,1)S(1)} %get-tuple-element.37), channel_id=1, source_target_pairs={{0,4},{4,0},{8,12},{12,8},{16,20},{20,16},{24,28},{28,24},{1,5},{5... | collective-permute-start | bytes 1572872 | tf_op jit(solution)/shard_map/ppermute | solution.py:22
  214.4 40.7 %collective-permute-start.53 = (bf16[3,256,2,128]{3,2,1,0:T(2,128)(2,1)S(1)}, bf16[3,256,2,128]{3,2,1,0:T(2,128)(2,1)S(1)}, u32[]{:S(2)}, u32[]{:S(2)}) collective-permute-start(bf16[3,256,2,128]{3,2,1,0:T(2,128)(2,1)S(1)} %get-tuple-element.47), channel_id=1, source_target_pairs={{0,4},{4,0},{8,12},{12,8},{16,20},{20,16},{24,28},{28,24},{1,5},{5... | collective-permute-start | bytes 1179656 | tf_op jit(solution)/shard_map/ppermute | solution.py:22
  227.7 25.3 %collective-permute-start.54 = (bf16[1,256,2,128]{3,2,1,0:T(2,128)(2,1)S(1)}, bf16[1,256,2,128]{3,2,1,0:T(2,128)(2,1)S(1)}, u32[]{:S(2)}, u32[]{:S(2)}) collective-permute-start(bf16[1,256,2,128]{3,2,1,0:T(2,128)(2,1)S(1)} %get-tuple-element.49), channel_id=1, source_target_pairs={{0,4},{4,0},{8,12},{12,8},{16,20},{20,16},{24,28},{28,24},{1,5},{5... | collective-permute-start | bytes 393224 | tf_op jit(solution)/shard_map/ppermute | solution.py:22
  230.5 23.0 %collective-permute-start.45 = (bf16[256,256]{1,0:T(8,128)(2,1)S(1)}, bf16[256,256]{1,0:T(8,128)(2,1)S(1)}, u32[]{:S(2)}, u32[]{:S(2)}) collective-permute-start(bf16[256,256]{1,0:T(8,128)(2,1)S(1)} %fusion.89), channel_id=1, source_target_pairs={{0,2},{1,3},{2,0},{3,1},{4,6},{5,7},{6,4},{7,5},{8,10},{9,11},{10,... | collective-permute-start | bytes 393224 | tf_op jit(solution)/shard_map/ppermute | solution.py:22
  232.1 34.5 %collective-permute-start.49 = (bf16[3,256,2,128]{3,2,1,0:T(2,128)(2,1)S(1)}, bf16[3,256,2,128]{3,2,1,0:T(2,128)(2,1)S(1)}, u32[]{:S(2)}, u32[]{:S(2)}) collective-permute-start(bf16[3,256,2,128]{3,2,1,0:T(2,128)(2,1)S(1)} %get-tuple-element.39), channel_id=1, source_target_pairs={{0,4},{4,0},{8,12},{12,8},{16,20},{20,16},{24,28},{28,24},{1,5},{5... | collective-permute-start | bytes 1179656 | tf_op jit(solution)/shard_map/ppermute | solution.py:22
  (43 other events, 490.2 us)
